TPU v7x, 256 devices: a whole 4x4x8 slice. The times are simulated.
256 devices in a mesh: row: 4 (over x_hi, core), col: 8 (over z), layer: 8 (over x_lo, y).
Axes of the slice: x: 4 (x_hi: 2, x_lo: 2; x = x_hi * 2 + x_lo), y: 4, z: 8, core: 2. Of those that a mesh axis runs over, the one named last changes fastest.
Arguments:
- amplitudes: float32 [12288, 16384], P(('row', 'col', 'layer')), may hold values from -6 to 6
- integrals: float32 [16384, 2048], P(('col', 'layer')), may hold values from -0.046875 to 0.046875
- pair_list: int32 [12288, 2], P(('row', 'col', 'layer')), may hold values from 0 to 199, as said below
- occupied_energy: float32 [200], replicated, may hold values from -1.5 to -0.3
- virtual_energy: float32 [2048], replicated, may hold values from 1 to 4
Outputs:
- ladder_update: float32 [12288, 2048], P(('row', 'col', 'layer'))
Inputs may be any that keep to these rules, and one draw needn't show every extreme that they name: `pair_list`: each row (i, j) holds two occupied orbital numbers with i <= j.
All inputs are finite; a program needn't handle non-finite values.
Results may differ from a plain program's by a relative error of at most 0.000071.
Values sent between devices are 32-bit elements; how exact they have to be, the bound alone decides.
No kernel may reach another device: no remote copies, remote signals or barrier semaphores. Data moves between devices by JAX's collectives and lax.ppermute only.
A program may use at most 128 MiB of HBM per device.

v0:
```python
import jax
import jax.numpy as jnp
from jax import lax
from jax.sharding import PartitionSpec as P


def energy_lookup(pair_list, occupied_energy):
    occ_index = jnp.arange(occupied_energy.shape[0], dtype=jnp.int32)
    occ_first = jnp.sum(
        jnp.where(pair_list[:, 0:1] == occ_index[None, :], occupied_energy[None, :], 0.0), axis=1
    )
    occ_second = jnp.sum(
        jnp.where(pair_list[:, 1:2] == occ_index[None, :], occupied_energy[None, :], 0.0), axis=1
    )
    return (occ_first, occ_second)


def body(amplitudes, integrals, pair_list, occupied_energy, virtual_energy):
    row_count = amplitudes.shape[0]
    col_count = lax.axis_size("col")
    integral_block = lax.all_gather(integrals, "layer", axis=0, tiled=True)
    shaped = amplitudes.reshape(row_count, col_count, amplitudes.shape[1] // col_count)
    partial_value = jnp.einsum(
        "rsk,kn->rsn",
        lax.all_to_all(shaped, "col", split_axis=1, concat_axis=1, tiled=True),
        integral_block,
        precision=lax.Precision.HIGHEST,
        preferred_element_type=jnp.float32,
    )
    returned = lax.all_to_all(partial_value, "col", split_axis=1, concat_axis=1, tiled=True)
    ladder = jnp.sum(returned, axis=1)
    occ_first, occ_second = energy_lookup(pair_list, occupied_energy)
    denominator = virtual_energy[None, :] - occ_first[:, None] - occ_second[:, None]
    return ladder / denominator


def solution(mesh):
    in_specs = (
        P(("row", "col", "layer"), None),
        P(("col", "layer"), None),
        P(("row", "col", "layer"), None),
        P(),
        P(),
    )
    out_specs = P(("row", "col", "layer"), None)
    return jax.shard_map(body, mesh=mesh, in_specs=in_specs, out_specs=out_specs, check_vma=False)
```

profile of v0, /device:TPU:1, one launch (start us, length us, event | category | flops | bytes accessed | tf_op | source)
XLA Modules:
  0.0 299.0 jit_solution(12691873429440723505)
XLA Ops:
  6.5 0.0 all-gather.2.cloned.1.call-start
  6.5 0.7 all-gather.2.cloned.1.call-update
  7.3 2.1 copy.18
  9.4 81.1 %all_to_all.10 = f32[48,8,2048]{2,0,1:T(8,128)S(1)} all-to-all(f32[48,8,2048]{2,0,1:T(8,128)S(1)} %bitcast.12), channel_id=1, replica_groups=mesh['row'=4,'col'=8,'layer'=8] {'col'}, dimensions={1} | all-to-all | bytes 6291456 | tf_op jit(solution)/shard_map/all_to_all | solution.py:25
  90.4 95.4 %all-gather.2.cloned.1.call-done = f32[2048,2048]{1,0:T(8,128)} async-done(((f32[256,2048]{1,0:T(8,128)}), f32[2048,2048]{1,0:T(8,128)}) %all-gather.2.cloned.1.call-update) | async-done | bytes 16777232 | tf_op jit(solution)/shard_map/all_gather | solution.py:21
  185.8 24.1 %fusion = f32[48,8,2048]{2,0,1:T(8,128)} fusion(f32[48,8,2048]{2,0,1:T(8,128)S(1)} %all_to_all.10, f32[2048,2048]{1,0:T(8,128)} %all-gather.2.cloned.1.call-done), kind=kOutput, calls=%fused_computation | convolution fusion | flops 19327352832 | bytes 23068672 | tf_op jit(solution)/shard_map/rsk,kn->rsn/dot_general | solution.py:23
  209.9 0.0 copy-start.2
  209.9 0.0 copy-start.1
  209.9 6.9 %all-to-all-start.1 = ((f32[48,8,2048]{2,0,1:T(8,128)}), f32[48,8,2048]{2,0,1:T(8,128)S(1)}, u32[]{:S(2)}, u32[]{:S(2)}) async-start(f32[48,8,2048]{2,0,1:T(8,128)} %fusion), calls=%async_computation.1 | async-start | bytes 6291456 | tf_op jit(solution)/shard_map/all_to_all | solution.py:30
  216.8 0.0 copy-done.2
  216.8 0.0 copy-start
  216.9 0.0 copy-done.1
  216.9 0.2 select_reduce_fusion.1
  217.0 74.0 %all-to-all-done.1 = f32[48,8,2048]{2,0,1:T(8,128)S(1)} async-done(((f32[48,8,2048]{2,0,1:T(8,128)}), f32[48,8,2048]{2,0,1:T(8,128)S(1)}, u32[]{:S(2)}, u32[]{:S(2)}) %all-to-all-start.1) | async-done | bytes 3145760 | tf_op jit(solution)/shard_map/all_to_all | solution.py:30
  291.1 0.2 reduce_sum.27
  291.3 0.0 copy-done
  291.3 0.9 subtract_divide_fusion
  (1 shorter events, 0.0 us)
Async XLA Ops:
  6.5 179.3 %all-gather.2.cloned.1.call-start = ((), (), s32[]{:S(2)}) async-start(), calls=%async_computation.2 | async-start | bytes 18874368 | tf_op jit(solution)/shard_map/all_gather | solution.py:21
  209.9 6.9 %copy-start.2 = (s32[48,2]{0,1:T(2,128)S(1)}, s32[48,2]{0,1:T(2,128)}, u32[]{:S(2)}) copy-start(s32[48,2]{0,1:T(2,128)} %param.7) | copy-start | bytes 1156
  209.9 6.9 %copy-start.1 = (f32[200]{0:T(256)S(1)}, f32[200]{0:T(256)}, u32[]{:S(2)}) copy-start(f32[200]{0:T(256)} %param.8) | copy-start | bytes 2404
  209.9 81.1 %all-to-all-start.1 = ((f32[48,8,2048]{2,0,1:T(8,128)}), f32[48,8,2048]{2,0,1:T(8,128)S(1)}, u32[]{:S(2)}, u32[]{:S(2)}) async-start(f32[48,8,2048]{2,0,1:T(8,128)} %fusion), calls=%async_computation.1 | async-start | bytes 6291456 | tf_op jit(solution)/shard_map/all_to_all | solution.py:30
  216.8 74.4 %copy-start = (f32[2048]{0:T(1024)S(1)}, f32[2048]{0:T(1024)}, u32[]{:S(2)}) copy-start(f32[2048]{0:T(1024)} %param.9) | copy-start | bytes 24580
Sparse Core Ops, SparseCore 0:
  9.1 176.6 all-gather.1
where the time goes:
time: 299 us
  waiting for transfers between devices  170 us (57%)
  blocking collectives  81.1 us (27%)
  matrix products  24.1 us (8%)
  between operations  13.4 us (4%)
  starting transfers between devices  6.88 us (2%)
    all_gather x1, waiting for transfers between devices, body(): integral_block = lax.all_gather(integrals, 'layer', axis=0, tiled=True)  95.4 us
    all_to_all x1, blocking collectives, body(): lax.all_to_all(shaped, 'col', split_axis=1, concat_axis=1, tiled=True)  81.1 us
    all_to_all x1, waiting for transfers between devices, body(): lax.all_to_all(partial_value, 'col', split_axis=1, concat_axis=1, tiled=T...  74 us
    dot_general x1, matrix products, body(): jnp.einsum('rsk,kn->rsn', lax.all_to_all(shaped, 'col', split_axis=1, con...  24.1 us
    all_to_all x1, starting transfers between devices, body(): lax.all_to_all(partial_value, 'col', split_axis=1, concat_axis=1, tiled=T...  6.88 us
  transfers between devices with their start and end apart: 2, of which 2 were waited for; matrix products, arithmetic and copies ran while one was open for 1% of the time, Pallas kernels for 0%

commit v1 on v0

v1 whole, which is shorter than its diff:
```python
import functools

import jax
import jax.numpy as jnp
from jax import lax
from jax.experimental import pallas as pl
from jax.experimental.pallas import tpu as pltpu
from jax.sharding import Mesh
from jax.sharding import PartitionSpec as P


AXES = ("xhi", "core", "z", "xlo", "y")
LAYERS = 8
RING = 8
CHAINS = (256, 256, 256, 256)
GROUPS = ((0, 1), (2, 3))


def energy_lookup(pair_list, occupied_energy):
    occ_index = jnp.arange(occupied_energy.shape[0], dtype=jnp.int32)
    occ_first = jnp.sum(
        jnp.where(pair_list[:, 0:1] == occ_index[None, :], occupied_energy[None, :], 0.0), axis=1
    )
    occ_second = jnp.sum(
        jnp.where(pair_list[:, 1:2] == occ_index[None, :], occupied_energy[None, :], 0.0), axis=1
    )
    return (occ_first, occ_second)


def shift(value, axis, step):
    count = lax.axis_size(axis)
    return lax.ppermute(value, axis, [(i, (i + step) % count) for i in range(count)])


def roll_kernel(z_ref, amp_ref, out_ref):
    depth = out_ref.shape[2]
    for layer in range(LAYERS):
        out_ref[layer] = amp_ref[:, layer * depth : (layer + 1) * depth]


def roll_amplitudes(amplitudes, z, depth):
    rows = amplitudes.shape[0]
    return pl.pallas_call(
        roll_kernel,
        grid_spec=pltpu.PrefetchScalarGridSpec(
            num_scalar_prefetch=1,
            grid=(RING,),
            in_specs=[
                pl.BlockSpec((rows, LAYERS * depth), lambda s, z_ref: (0, lax.rem(z_ref[0] + s, RING)))
            ],
            out_specs=pl.BlockSpec((LAYERS, rows, depth), lambda s, z_ref: (0, 0, s)),
        ),
        out_shape=jax.ShapeDtypeStruct((LAYERS, rows, RING * depth), jnp.float32),
        cost_estimate=pl.CostEstimate(flops=0, bytes_accessed=8 * amplitudes.size, transcendentals=0),
        name="roll",
    )(z, amplitudes)


def split(value):
    high = value.astype(jnp.bfloat16)
    low = (value - high.astype(jnp.float32)).astype(jnp.bfloat16)
    return high, low


def product_kernel(places, core_ref, own_ref, other_ref, *refs):
    blocks, out_ref, high_ref, low_ref = refs[:-3], refs[-3], refs[-2], refs[-1]
    rows = own_ref.shape[0]
    for (offset, column), block in zip(places, blocks):
        high, low = split(block[...])
        depth, width = block.shape
        high_ref[offset : offset + depth, column : column + width] = high
        low_ref[offset : offset + depth, column : column + width] = low
    dot = functools.partial(jnp.dot, preferred_element_type=jnp.float32)
    core = core_ref[0]
    for left_ref, place in ((own_ref, core), (other_ref, 1 - core)):
        high, low = split(left_ref[...])
        start = pl.multiple_of(place * rows, rows)
        out_ref[pl.ds(start, rows), :] = (
            dot(high, low_ref[...]) + dot(low, high_ref[...]) + dot(high, high_ref[...])
        )


def product(own, other, core, blocks, places, width):
    rows, depth = own.shape
    vmem = pl.BlockSpec(memory_space=pltpu.VMEM)
    return pl.pallas_call(
        functools.partial(product_kernel, places),
        in_specs=[pl.BlockSpec(memory_space=pltpu.SMEM)] + [vmem] * (2 + len(blocks)),
        out_specs=vmem,
        scratch_shapes=[
            pltpu.VMEM((depth, width), jnp.bfloat16),
            pltpu.VMEM((depth, width), jnp.bfloat16),
        ],
        out_shape=jax.ShapeDtypeStruct((2 * rows, width), jnp.float32),
        compiler_params=pltpu.CompilerParams(vmem_limit_bytes=40 * 1024 * 1024),
        cost_estimate=pl.CostEstimate(
            flops=12 * rows * depth * width, bytes_accessed=8 * rows * depth, transcendentals=0
        ),
        name="product",
    )(core, own, other, *blocks)


def body(amplitudes, integrals, pair_list, occupied_energy, virtual_energy):
    rows = amplitudes.shape[0]
    depth, cols = integrals.shape
    core = lax.axis_index("core")
    z = lax.axis_index("z")
    half = cols // 2
    chains = []
    start = 0
    for n, width in enumerate(CHAINS):
        block = lax.dynamic_slice(integrals, (0, core * half + start), (depth, width))
        plus = [block]
        minus = [block]
        ahead = 4 - n % 2
        for _ in range(1, ahead + 1):
            plus.append(shift(plus[-1], "z", -1))
        for _ in range(1, RING - ahead):
            minus.append(shift(minus[-1], "z", 1))
        chains.append(plus + minus[:0:-1])
        start += width
    send = roll_amplitudes(amplitudes, z[None], depth)
    got = lax.all_to_all(send, ("xlo", "y"), split_axis=0, concat_axis=0, tiled=True)
    own = got.reshape(LAYERS * rows, RING * depth)
    other = lax.ppermute(own, "core", [(0, 1), (1, 0)])
    offsets = [s * depth for s in range(RING)]
    sums = []
    for group in GROUPS:
        blocks, places, width = [], [], 0
        for n in group:
            blocks += chains[n]
            places += [(offset, width) for offset in offsets]
            width += CHAINS[n]
        partial = product(own, other, core[None], blocks, tuple(places), width)
        back = lax.all_to_all(
            partial.reshape(2 * LAYERS, rows, width), ("core", "xlo", "y"),
            split_axis=0, concat_axis=0, tiled=True,
        )
        sums.append(jnp.sum(back.reshape(2, LAYERS, rows, width), axis=1))
    ladder = jnp.concatenate([s[c] for c in range(2) for s in sums], axis=1)
    occ_first, occ_second = energy_lookup(pair_list, occupied_energy)
    denominator = virtual_energy[None, :] - occ_first[:, None] - occ_second[:, None]
    return ladder / denominator


def solution(mesh):
    fine = Mesh(mesh.devices.reshape(2, 2, 8, 2, 4), AXES)
    rows = P(AXES, None)
    in_specs = (rows, P(("z", "xlo", "y"), None), rows, P(), P())

    return jax.shard_map(body, mesh=fine, in_specs=in_specs, out_specs=rows, check_vma=False)
```

time: 299 us -> 189 us (0.63)
  waiting for transfers between devices: 170 us -> 59.8 us
  starting transfers between devices: 6.88 us -> 57.8 us
  blocking collectives: 81.1 us -> 43 us
  matrix products: 24.1 us -> 0 us
  Pallas kernels: 0 us -> 20.3 us
  between operations: 13.4 us -> 0.13 us
    all_gather x1 -> x0, waiting for transfers between devices: 95.4 us -> none  [body(): integral_block = lax.all_gather(integrals, 'layer', axis=0, tiled=True)]
    all_to_all x1 -> x2, waiting for transfers between devices: 74 us -> 20.1 us  [body(): lax.all_to_all(partial.reshape(2 * LAYERS, rows, width), ('core', 'xlo',...]
    ppermute x0 -> x29, starting transfers between devices: none -> 43.9 us  [the longest x28 41.5 us: shift(): lax.ppermute(value, axis, [(i, (i + step) % count) for i in range(count)])]
    ppermute x0 -> x29, waiting for transfers between devices: none -> 39.7 us  [the longest x28 39.7 us: shift(): lax.ppermute(value, axis, [(i, (i + step) % count) for i in range(count)])]
    all_to_all x1, blocking collectives: 81.1 us -> 43 us  [body(): lax.all_to_all(send, ('xlo', 'y'), split_axis=0, concat_axis=0, tiled=True)]
    dot_general x1 -> x0, matrix products: 24.1 us -> none  [body(): jnp.einsum('rsk,kn->rsn', lax.all_to_all(shaped, 'col', split_axis=1, con...]
    pallas_call x0 -> x3, Pallas kernels: none -> 20.3 us  [the longest x2 14.1 us: product(): pl.pallas_call(functools.partial(product_kernel, places), in_specs=[pl.Bl...]
    all_to_all x1 -> x2, starting transfers between devices: 6.88 us -> 13.9 us  [body(): lax.all_to_all(partial.reshape(2 * LAYERS, rows, width), ('core', 'xlo',...]
  transfers between devices with their start and end apart: 2 -> 31, of which waited for: 2 -> 17; matrix products, arithmetic and copies ran while one was open for 1% -> 2% of each run, Pallas kernels for 0% -> 7%
where the time goes in v1:
time: 189 us; the launch traced here: 188 us
  waiting for transfers between devices  59.8 us (32%)
  starting transfers between devices  57.8 us (31%)
  blocking collectives  43 us (23%)
  Pallas kernels  20.3 us (11%)
  local copies, waits for them, and re-layouts  4.42 us (2%)
  other arithmetic  2.76 us (1%)
    all_to_all x1, blocking collectives, body(): lax.all_to_all(send, ('xlo', 'y'), split_axis=0, concat_axis=0, tiled=True)  43 us
    ppermute x28, starting transfers between devices, shift(): lax.ppermute(value, axis, [(i, (i + step) % count) for i in range(count)])  41.5 us
    ppermute x28, waiting for transfers between devices, shift(): lax.ppermute(value, axis, [(i, (i + step) % count) for i in range(count)])  39.7 us
    all_to_all x2, waiting for transfers between devices, body(): lax.all_to_all(partial.reshape(2 * LAYERS, rows, width), ('core', 'xlo',...  20.1 us
    pallas_call x2, Pallas kernels, product(): pl.pallas_call(functools.partial(product_kernel, places), in_specs=[pl.Bl...  14.1 us
    all_to_all x2, starting transfers between devices, body(): lax.all_to_all(partial.reshape(2 * LAYERS, rows, width), ('core', 'xlo',...  13.9 us
    pallas_call x1, Pallas kernels, roll_amplitudes(): pl.pallas_call(roll_kernel, grid_spec=pltpu.PrefetchScalarGridSpec(num_sc...  6.23 us
  transfers between devices with their start and end apart: 31, of which 17 were waited for; matrix products, arithmetic and copies ran while one was open for 2% of the time, Pallas kernels for 7%

profile of v1, /device:TPU:1, one launch (start us, length us, event | category | flops | bytes accessed | tf_op | source)
XLA Modules:
  0.0 188.3 jit_solution(6694636810201533079)
XLA Ops:
  0.0 6.2 %roll.1 = f32[8,48,2048]{2,1,0:T(8,128)} custom-call(s32[1]{0:T(128)} %bitcast.1.z_ref, f32[48,16384]{1,0:T(8,128)} %amp_ref.1), custom_call_target="tpu_custom_call" | custom-call | bytes 6291456 | tf_op jit(solution)/shard_map/roll/pallas_call | solution.py:43
  6.2 43.0 %all_to_all.15 = f32[8,48,2048]{2,1,0:T(8,128)S(1)} all-to-all(f32[8,48,2048]{2,1,0:T(8,128)} %roll.1), channel_id=1, replica_groups=mesh['xhi'=2,'core'=2,'z'=8,'xlo'=2,'y'=4] {'xlo','y'}, dimensions={0} | all-to-all | bytes 6291456 | tf_op jit(solution)/shard_map/all_to_all | solution.py:123
  49.3 2.4 %collective-permute-start = (f32[384,2048]{1,0:T(8,128)S(1)}, f32[384,2048]{1,0:T(8,128)}, u32[]{:S(2)}, u32[]{:S(2)}) collective-permute-start(f32[384,2048]{1,0:T(8,128)S(1)} %bitcast.21), channel_id=1, source_target_pairs={{0,64},{64,0},{1,65},{65,1},{2,66},{66,2},{3,67},{67,3},{4,68},{68... | collective-permute-start | bytes 9437192 | tf_op jit(solution)/shard_map/ppermute | solution.py:125
  51.7 2.0 %constant_dynamic-slice_fusion.2 = (f32[256,256]{1,0:T(8,128)S(1)}, f32[256,256]{1,0:T(8,128)S(1)}, f32[256,256]{1,0:T(8,128)S(1)}, f32[256,256]{1,0:T(8,128)}) fusion(f32[256,2048]{1,0:T(8,128)} %param.6, s32[]{:T(128)S(6)} %select_n.20, s32[]{:T(128)S(6)} %select_n.19, s32[]{:T(128)S(6)} %select_n.22, s32[]{:T(128)S(6)} %select_n.21), kind=kLoop, calls=%fused_computation.13 | loop fusion | bytes 2097168 | tf_op jit(solution)/shard_map/dynamic_slice | solution.py:112
  53.7 1.6 collective-permute-start.11
  55.3 3.9 %collective-permute-start.1 = (f32[256,256]{1,0:T(8,128)S(1)}, f32[256,256]{1,0:T(8,128)S(1)}, u32[]{:S(2)}, u32[]{:S(2)}) collective-permute-start(f32[256,256]{1,0:T(8,128)S(1)} %get-tuple-element.8.refs_0_), channel_id=1, source_target_pairs={{0,56},{8,0},{16,8},{24,16},{32,24},{40,32},{48,40},{56,48},{1,57}... | collective-permute-start | bytes 786440 | tf_op jit(solution)/shard_map/ppermute | solution.py:32
  59.2 1.5 collective-permute-start.8
  60.7 0.0 collective-permute-start.5
  60.7 5.2 %collective-permute-done.11.refs_15_ = f32[256,256]{1,0:T(8,128)S(1)} collective-permute-done((f32[256,256]{1,0:T(8,128)S(1)}, f32[256,256]{1,0:T(8,128)S(1)}, u32[]{:S(2)}, u32[]{:S(2)}) %collective-permute-start.11) | collective-permute-done | bytes 262176 | tf_op jit(solution)/shard_map/ppermute | solution.py:32
  65.9 0.0 collective-permute-start.12
  65.9 0.0 collective-permute-done.1.refs_1_
  65.9 2.7 %collective-permute-start.2 = (f32[256,256]{1,0:T(8,128)S(1)}, f32[256,256]{1,0:T(8,128)S(1)}, u32[]{:S(2)}, u32[]{:S(2)}) collective-permute-start(f32[256,256]{1,0:T(8,128)S(1)} %collective-permute-done.1.refs_1_), channel_id=1, source_target_pairs={{0,56},{8,0},{16,8},{24,16},{32,24},{40,32},{48,40},{56,48},{1,57}... | collective-permute-start | bytes 786440 | tf_op jit(solution)/shard_map/ppermute | solution.py:32
  68.6 1.9 %collective-permute-done.8.refs_9_ = f32[256,256]{1,0:T(8,128)S(1)} collective-permute-done((f32[256,256]{1,0:T(8,128)S(1)}, f32[256,256]{1,0:T(8,128)S(1)}, u32[]{:S(2)}, u32[]{:S(2)}) %collective-permute-start.8) | collective-permute-done | bytes 262176 | tf_op jit(solution)/shard_map/ppermute | solution.py:32
  70.5 3.4 %collective-permute-start.9 = (f32[256,256]{1,0:T(8,128)S(1)}, f32[256,256]{1,0:T(8,128)S(1)}, u32[]{:S(2)}, u32[]{:S(2)}) collective-permute-start(f32[256,256]{1,0:T(8,128)S(1)} %collective-permute-done.8.refs_9_), channel_id=1, source_target_pairs={{0,56},{8,0},{16,8},{24,16},{32,24},{40,32},{48,40},{56,48},{1,57}... | collective-permute-start | bytes 786440 | tf_op jit(solution)/shard_map/ppermute | solution.py:32
  73.9 0.0 collective-permute-done.5.refs_7_
  73.9 0.0 collective-permute-start.6
  73.9 3.2 %collective-permute-done.12.refs_14_ = f32[256,256]{1,0:T(8,128)S(1)} collective-permute-done((f32[256,256]{1,0:T(8,128)S(1)}, f32[256,256]{1,0:T(8,128)S(1)}, u32[]{:S(2)}, u32[]{:S(2)}) %collective-permute-start.12) | collective-permute-done | bytes 262176 | tf_op jit(solution)/shard_map/ppermute | solution.py:32
  77.2 0.0 collective-permute-start.13
  77.2 0.0 collective-permute-done.2.refs_2_
  77.2 2.7 %collective-permute-start.3 = (f32[256,256]{1,0:T(8,128)S(1)}, f32[256,256]{1,0:T(8,128)S(1)}, u32[]{:S(2)}, u32[]{:S(2)}) collective-permute-start(f32[256,256]{1,0:T(8,128)S(1)} %collective-permute-done.2.refs_2_), channel_id=1, source_target_pairs={{0,56},{8,0},{16,8},{24,16},{32,24},{40,32},{48,40},{56,48},{1,57}... | collective-permute-start | bytes 786440 | tf_op jit(solution)/shard_map/ppermute | solution.py:32
  79.8 1.9 %collective-permute-done.9.refs_10_ = f32[256,256]{1,0:T(8,128)S(1)} collective-permute-done((f32[256,256]{1,0:T(8,128)S(1)}, f32[256,256]{1,0:T(8,128)S(1)}, u32[]{:S(2)}, u32[]{:S(2)}) %collective-permute-start.9) | collective-permute-done | bytes 262176 | tf_op jit(solution)/shard_map/ppermute | solution.py:32
  81.8 3.4 %collective-permute-start.10 = (f32[256,256]{1,0:T(8,128)S(1)}, f32[256,256]{1,0:T(8,128)S(1)}, u32[]{:S(2)}, u32[]{:S(2)}) collective-permute-start(f32[256,256]{1,0:T(8,128)S(1)} %collective-permute-done.9.refs_10_), channel_id=1, source_target_pairs={{0,56},{8,0},{16,8},{24,16},{32,24},{40,32},{48,40},{56,48},{1,57}... | collective-permute-start | bytes 786440 | tf_op jit(solution)/shard_map/ppermute | solution.py:32
  85.2 0.0 collective-permute-done.6.refs_6_
  85.2 0.0 collective-permute-start.7
  85.2 1.9 collective-permute-done.13.refs_13_
  87.0 0.0 collective-permute-start.14
  87.0 0.3 collective-permute-done.3.refs_3_
  87.4 3.4 %collective-permute-start.4 = (f32[256,256]{1,0:T(8,128)S(1)}, f32[256,256]{1,0:T(8,128)S(1)}, u32[]{:S(2)}, u32[]{:S(2)}) collective-permute-start(f32[256,256]{1,0:T(8,128)S(1)} %collective-permute-done.3.refs_3_), channel_id=1, source_target_pairs={{0,56},{8,0},{16,8},{24,16},{32,24},{40,32},{48,40},{56,48},{1,57}... | collective-permute-start | bytes 786440 | tf_op jit(solution)/shard_map/ppermute | solution.py:32
  90.8 2.2 %collective-permute-done.10.refs_11_ = f32[256,256]{1,0:T(8,128)S(1)} collective-permute-done((f32[256,256]{1,0:T(8,128)S(1)}, f32[256,256]{1,0:T(8,128)S(1)}, u32[]{:S(2)}, u32[]{:S(2)}) %collective-permute-start.10) | collective-permute-done | bytes 262176 | tf_op jit(solution)/shard_map/ppermute | solution.py:32
  93.0 3.4 %collective-permute-start.15 = (f32[256,256]{1,0:T(8,128)}, f32[256,256]{1,0:T(8,128)}, u32[]{:S(2)}, u32[]{:S(2)}) collective-permute-start(f32[256,256]{1,0:T(8,128)} %get-tuple-element.10.refs_0_), channel_id=1, source_target_pairs={{0,56},{8,0},{16,8},{24,16},{32,24},{40,32},{48,40},{56,48},{1,57}... | collective-permute-start | bytes 786440 | tf_op jit(solution)/shard_map/ppermute | solution.py:32
  96.4 0.0 collective-permute-done.7.refs_5_
  96.4 0.0 collective-permute-start.25
  96.4 1.9 collective-permute-done.14.refs_12_
  98.3 0.3 collective-permute-done.4.refs_4_
  98.6 6.9 %product.2 = f32[768,512]{1,0:T(8,128)S(1)} custom-call(s32[1]{0:T(128)} %bitcast.core_ref, f32[384,2048]{1,0:T(8,128)S(1)} %bitcast.22, f32[384,2048]{1,0:T(8,128)} %collective-permute-done.other_ref, f32[256,256]{1,0:T(8,128)S(1)} %get-tuple-element.8.refs_0_, f32[256,256]{1,0:T(8,128)S(1)} %collective-permute-done.1.refs_1_, ...), custom_call_target="tpu_custom_call" | custom-call | flops 4831838208 | bytes 6291456 | tf_op jit(solution)/shard_map/product/pallas_call | solution.py:86
  105.6 1.2 copy-done
  106.7 6.3 %all-to-all-start.1 = ((f32[16,48,512]{2,1,0:T(8,128)}), f32[16,48,512]{2,1,0:T(8,128)}, u32[]{:S(2)}, u32[]{:S(2)}) async-start(f32[16,48,512]{2,1,0:T(8,128)} %bitcast.24), calls=%async_computation.1 | async-start | bytes 3145728 | tf_op jit(solution)/shard_map/all_to_all | solution.py:135
  113.1 2.7 %collective-permute-start.22 = (f32[256,256]{1,0:T(8,128)S(1)}, f32[256,256]{1,0:T(8,128)S(1)}, u32[]{:S(2)}, u32[]{:S(2)}) collective-permute-start(f32[256,256]{1,0:T(8,128)S(1)} %get-tuple-element.9.refs_8_), channel_id=1, source_target_pairs={{0,56},{8,0},{16,8},{24,16},{32,24},{40,32},{48,40},{56,48},{1,57}... | collective-permute-start | bytes 786440 | tf_op jit(solution)/shard_map/ppermute | solution.py:32
  115.7 0.0 collective-permute-done.15.refs_1_
  115.8 1.4 collective-permute-start.16
  117.1 0.1 collective-permute-start.26
  117.2 4.9 %collective-permute-done.19.refs_7_ = f32[256,256]{1,0:T(8,128)S(1)} collective-permute-done((f32[256,256]{1,0:T(8,128)}, f32[256,256]{1,0:T(8,128)S(1)}, u32[]{:S(2)}, u32[]{:S(2)}) %collective-permute-start.19) | collective-permute-done | bytes 262176 | tf_op jit(solution)/shard_map/ppermute | solution.py:32
  122.1 2.7 %collective-permute-start.23 = (f32[256,256]{1,0:T(8,128)S(1)}, f32[256,256]{1,0:T(8,128)S(1)}, u32[]{:S(2)}, u32[]{:S(2)}) collective-permute-start(f32[256,256]{1,0:T(8,128)S(1)} %collective-permute-done.22.refs_9_), channel_id=1, source_target_pairs={{0,56},{8,0},{16,8},{24,16},{32,24},{40,32},{48,40},{56,48},{1,57}... | collective-permute-start | bytes 786440 | tf_op jit(solution)/shard_map/ppermute | solution.py:32
  124.8 2.2 %collective-permute-done.16.refs_2_ = f32[256,256]{1,0:T(8,128)S(1)} collective-permute-done((f32[256,256]{1,0:T(8,128)}, f32[256,256]{1,0:T(8,128)S(1)}, u32[]{:S(2)}, u32[]{:S(2)}) %collective-permute-start.16) | collective-permute-done | bytes 262176 | tf_op jit(solution)/shard_map/ppermute | solution.py:32
  127.0 3.0 %collective-permute-start.17 = (f32[256,256]{1,0:T(8,128)S(1)}, f32[256,256]{1,0:T(8,128)S(1)}, u32[]{:S(2)}, u32[]{:S(2)}) collective-permute-start(f32[256,256]{1,0:T(8,128)S(1)} %collective-permute-done.16.refs_2_), channel_id=1, source_target_pairs={{0,56},{8,0},{16,8},{24,16},{32,24},{40,32},{48,40},{56,48},{1,57}... | collective-permute-start | bytes 786440 | tf_op jit(solution)/shard_map/ppermute | solution.py:32
  129.9 0.0 collective-permute-done.26.refs_14_
  130.0 3.4 %collective-permute-done.20.refs_6_ = f32[256,256]{1,0:T(8,128)S(1)} collective-permute-done((f32[256,256]{1,0:T(8,128)S(1)}, f32[256,256]{1,0:T(8,128)S(1)}, u32[]{:S(2)}, u32[]{:S(2)}) %collective-permute-start.20) | collective-permute-done | bytes 262176 | tf_op jit(solution)/shard_map/ppermute | solution.py:32
  133.4 0.0 collective-permute-start.21
  133.4 0.0 collective-permute-done.23.refs_10_
  133.4 2.7 %collective-permute-start.24 = (f32[256,256]{1,0:T(8,128)S(1)}, f32[256,256]{1,0:T(8,128)S(1)}, u32[]{:S(2)}, u32[]{:S(2)}) collective-permute-start(f32[256,256]{1,0:T(8,128)S(1)} %collective-permute-done.23.refs_10_), channel_id=1, source_target_pairs={{0,56},{8,0},{16,8},{24,16},{32,24},{40,32},{48,40},{56,48},{1,57}... | collective-permute-start | bytes 786440 | tf_op jit(solution)/shard_map/ppermute | solution.py:32
  136.0 2.1 %collective-permute-done.17.refs_3_ = f32[256,256]{1,0:T(8,128)S(1)} collective-permute-done((f32[256,256]{1,0:T(8,128)S(1)}, f32[256,256]{1,0:T(8,128)S(1)}, u32[]{:S(2)}, u32[]{:S(2)}) %collective-permute-start.17) | collective-permute-done | bytes 262176 | tf_op jit(solution)/shard_map/ppermute | solution.py:32
  138.1 3.0 %collective-permute-start.18 = (f32[256,256]{1,0:T(8,128)S(1)}, f32[256,256]{1,0:T(8,128)S(1)}, u32[]{:S(2)}, u32[]{:S(2)}) collective-permute-start(f32[256,256]{1,0:T(8,128)S(1)} %collective-permute-done.17.refs_3_), channel_id=1, source_target_pairs={{0,56},{8,0},{16,8},{24,16},{32,24},{40,32},{48,40},{56,48},{1,57}... | collective-permute-start | bytes 786440 | tf_op jit(solution)/shard_map/ppermute | solution.py:32
  141.1 1.8 collective-permute-done.21.refs_5_
  142.9 0.8 collective-permute-done.24.refs_11_
  143.7 5.6 %collective-permute-done.18.refs_4_ = f32[256,256]{1,0:T(8,128)S(1)} collective-permute-done((f32[256,256]{1,0:T(8,128)S(1)}, f32[256,256]{1,0:T(8,128)S(1)}, u32[]{:S(2)}, u32[]{:S(2)}) %collective-permute-start.18) | collective-permute-done | bytes 262176 | tf_op jit(solution)/shard_map/ppermute | solution.py:32
  149.4 7.2 %product.3 = f32[768,512]{1,0:T(8,128)S(1)} custom-call(s32[1]{0:T(128)} %bitcast.core_ref, f32[384,2048]{1,0:T(8,128)S(1)} %bitcast.23, f32[384,2048]{1,0:T(8,128)} %collective-permute-done.other_ref, f32[256,256]{1,0:T(8,128)} %get-tuple-element.10.refs_0_, f32[256,256]{1,0:T(8,128)} %collective-permute-done.15.refs_1_, ...), custom_call_target="tpu_custom_call" | custom-call | flops 4831838208 | bytes 6291456 | tf_op jit(solution)/shard_map/product/pallas_call | solution.py:86
  156.5 1.2 copy-done.1
  157.7 7.6 %all-to-all-start.2 = ((f32[16,48,512]{2,1,0:T(8,128)}), f32[16,48,512]{2,1,0:T(8,128)S(1)}, u32[]{:S(2)}, u32[]{:S(2)}) async-start(f32[16,48,512]{2,1,0:T(8,128)} %bitcast.25), calls=%async_computation.2 | async-start | bytes 3145728 | tf_op jit(solution)/shard_map/all_to_all | solution.py:135
  165.4 0.2 select_reduce_fusion.1
  165.5 0.0 copy-start.2
  165.6 1.6 bitcast_reduce_fusion.1
  167.1 20.1 %all-to-all-done.2 = f32[16,48,512]{2,1,0:T(8,128)S(1)} async-done(((f32[16,48,512]{2,1,0:T(8,128)}), f32[16,48,512]{2,1,0:T(8,128)S(1)}, u32[]{:S(2)}, u32[]{:S(2)}) %all-to-all-start.2) | async-done | bytes 1572896 | tf_op jit(solution)/shard_map/all_to_all | solution.py:135
  187.2 0.1 bitcast_reduce_fusion
  187.4 0.9 maximum_divide_fusion
  (20 shorter events, 0.1 us)
Async XLA Ops:
  49.3 49.3 %collective-permute-start = (f32[384,2048]{1,0:T(8,128)S(1)}, f32[384,2048]{1,0:T(8,128)}, u32[]{:S(2)}, u32[]{:S(2)}) collective-permute-start(f32[384,2048]{1,0:T(8,128)S(1)} %bitcast.21), channel_id=1, source_target_pairs={{0,64},{64,0},{1,65},{65,1},{2,66},{66,2},{3,67},{67,3},{4,68},{68... | collective-permute-start | bytes 9437192 | tf_op jit(solution)/shard_map/ppermute | solution.py:125
  53.7 12.3 %collective-permute-start.11 = (f32[256,256]{1,0:T(8,128)S(1)}, f32[256,256]{1,0:T(8,128)S(1)}, u32[]{:S(2)}, u32[]{:S(2)}) collective-permute-start(f32[256,256]{1,0:T(8,128)S(1)} %get-tuple-element.7.refs_8_), channel_id=1, source_target_pairs={{0,8},{8,16},{16,24},{24,32},{32,40},{40,48},{48,56},{56,0},{1,9},... | collective-permute-start | bytes 786440 | tf_op jit(solution)/shard_map/ppermute | solution.py:32
  55.3 10.6 %collective-permute-start.1 = (f32[256,256]{1,0:T(8,128)S(1)}, f32[256,256]{1,0:T(8,128)S(1)}, u32[]{:S(2)}, u32[]{:S(2)}) collective-permute-start(f32[256,256]{1,0:T(8,128)S(1)} %get-tuple-element.8.refs_0_), channel_id=1, source_target_pairs={{0,56},{8,0},{16,8},{24,16},{32,24},{40,32},{48,40},{56,48},{1,57}... | collective-permute-start | bytes 786440 | tf_op jit(solution)/shard_map/ppermute | solution.py:32
  59.2 11.3 %collective-permute-start.8 = (f32[256,256]{1,0:T(8,128)S(1)}, f32[256,256]{1,0:T(8,128)S(1)}, u32[]{:S(2)}, u32[]{:S(2)}) collective-permute-start(f32[256,256]{1,0:T(8,128)S(1)} %get-tuple-element.7.refs_8_), channel_id=1, source_target_pairs={{0,56},{8,0},{16,8},{24,16},{32,24},{40,32},{48,40},{56,48},{1,57}... | collective-permute-start | bytes 786440 | tf_op jit(solution)/shard_map/ppermute | solution.py:32
  60.7 13.2 %collective-permute-start.5 = (f32[256,256]{1,0:T(8,128)S(1)}, f32[256,256]{1,0:T(8,128)S(1)}, u32[]{:S(2)}, u32[]{:S(2)}) collective-permute-start(f32[256,256]{1,0:T(8,128)S(1)} %get-tuple-element.8.refs_0_), channel_id=1, source_target_pairs={{0,8},{8,16},{16,24},{24,32},{32,40},{40,48},{48,56},{56,0},{1,9},... | collective-permute-start | bytes 786440 | tf_op jit(solution)/shard_map/ppermute | solution.py:32
  65.9 11.2 %collective-permute-start.12 = (f32[256,256]{1,0:T(8,128)S(1)}, f32[256,256]{1,0:T(8,128)S(1)}, u32[]{:S(2)}, u32[]{:S(2)}) collective-permute-start(f32[256,256]{1,0:T(8,128)S(1)} %collective-permute-done.11.refs_15_), channel_id=1, source_target_pairs={{0,8},{8,16},{16,24},{24,32},{32,40},{40,48},{48,56},{56,0},{1,9},... | collective-permute-start | bytes 786440 | tf_op jit(solution)/shard_map/ppermute | solution.py:32
  65.9 11.2 %collective-permute-start.2 = (f32[256,256]{1,0:T(8,128)S(1)}, f32[256,256]{1,0:T(8,128)S(1)}, u32[]{:S(2)}, u32[]{:S(2)}) collective-permute-start(f32[256,256]{1,0:T(8,128)S(1)} %collective-permute-done.1.refs_1_), channel_id=1, source_target_pairs={{0,56},{8,0},{16,8},{24,16},{32,24},{40,32},{48,40},{56,48},{1,57}... | collective-permute-start | bytes 786440 | tf_op jit(solution)/shard_map/ppermute | solution.py:32
  70.5 11.2 %collective-permute-start.9 = (f32[256,256]{1,0:T(8,128)S(1)}, f32[256,256]{1,0:T(8,128)S(1)}, u32[]{:S(2)}, u32[]{:S(2)}) collective-permute-start(f32[256,256]{1,0:T(8,128)S(1)} %collective-permute-done.8.refs_9_), channel_id=1, source_target_pairs={{0,56},{8,0},{16,8},{24,16},{32,24},{40,32},{48,40},{56,48},{1,57}... | collective-permute-start | bytes 786440 | tf_op jit(solution)/shard_map/ppermute | solution.py:32
  73.9 11.2 %collective-permute-start.6 = (f32[256,256]{1,0:T(8,128)S(1)}, f32[256,256]{1,0:T(8,128)S(1)}, u32[]{:S(2)}, u32[]{:S(2)}) collective-permute-start(f32[256,256]{1,0:T(8,128)S(1)} %collective-permute-done.5.refs_7_), channel_id=1, source_target_pairs={{0,8},{8,16},{16,24},{24,32},{32,40},{40,48},{48,56},{56,0},{1,9},... | collective-permute-start | bytes 786440 | tf_op jit(solution)/shard_map/ppermute | solution.py:32
  77.2 9.9 %collective-permute-start.13 = (f32[256,256]{1,0:T(8,128)S(1)}, f32[256,256]{1,0:T(8,128)S(1)}, u32[]{:S(2)}, u32[]{:S(2)}) collective-permute-start(f32[256,256]{1,0:T(8,128)S(1)} %collective-permute-done.12.refs_14_), channel_id=1, source_target_pairs={{0,8},{8,16},{16,24},{24,32},{32,40},{40,48},{48,56},{56,0},{1,9},... | collective-permute-start | bytes 786440 | tf_op jit(solution)/shard_map/ppermute | solution.py:32
  77.2 10.2 %collective-permute-start.3 = (f32[256,256]{1,0:T(8,128)S(1)}, f32[256,256]{1,0:T(8,128)S(1)}, u32[]{:S(2)}, u32[]{:S(2)}) collective-permute-start(f32[256,256]{1,0:T(8,128)S(1)} %collective-permute-done.2.refs_2_), channel_id=1, source_target_pairs={{0,56},{8,0},{16,8},{24,16},{32,24},{40,32},{48,40},{56,48},{1,57}... | collective-permute-start | bytes 786440 | tf_op jit(solution)/shard_map/ppermute | solution.py:32
  81.8 11.2 %collective-permute-start.10 = (f32[256,256]{1,0:T(8,128)S(1)}, f32[256,256]{1,0:T(8,128)S(1)}, u32[]{:S(2)}, u32[]{:S(2)}) collective-permute-start(f32[256,256]{1,0:T(8,128)S(1)} %collective-permute-done.9.refs_10_), channel_id=1, source_target_pairs={{0,56},{8,0},{16,8},{24,16},{32,24},{40,32},{48,40},{56,48},{1,57}... | collective-permute-start | bytes 786440 | tf_op jit(solution)/shard_map/ppermute | solution.py:32
  85.2 11.2 %collective-permute-start.7 = (f32[256,256]{1,0:T(8,128)S(1)}, f32[256,256]{1,0:T(8,128)S(1)}, u32[]{:S(2)}, u32[]{:S(2)}) collective-permute-start(f32[256,256]{1,0:T(8,128)S(1)} %collective-permute-done.6.refs_6_), channel_id=1, source_target_pairs={{0,8},{8,16},{16,24},{24,32},{32,40},{40,48},{48,56},{56,0},{1,9},... | collective-permute-start | bytes 786440 | tf_op jit(solution)/shard_map/ppermute | solution.py:32
  87.0 11.2 %collective-permute-start.14 = (f32[256,256]{1,0:T(8,128)S(1)}, f32[256,256]{1,0:T(8,128)S(1)}, u32[]{:S(2)}, u32[]{:S(2)}) collective-permute-start(f32[256,256]{1,0:T(8,128)S(1)} %collective-permute-done.13.refs_13_), channel_id=1, source_target_pairs={{0,8},{8,16},{16,24},{24,32},{32,40},{40,48},{48,56},{56,0},{1,9},... | collective-permute-start | bytes 786440 | tf_op jit(solution)/shard_map/ppermute | solution.py:32
  87.4 11.2 %collective-permute-start.4 = (f32[256,256]{1,0:T(8,128)S(1)}, f32[256,256]{1,0:T(8,128)S(1)}, u32[]{:S(2)}, u32[]{:S(2)}) collective-permute-start(f32[256,256]{1,0:T(8,128)S(1)} %collective-permute-done.3.refs_3_), channel_id=1, source_target_pairs={{0,56},{8,0},{16,8},{24,16},{32,24},{40,32},{48,40},{56,48},{1,57}... | collective-permute-start | bytes 786440 | tf_op jit(solution)/shard_map/ppermute | solution.py:32
  93.0 22.8 %collective-permute-start.15 = (f32[256,256]{1,0:T(8,128)}, f32[256,256]{1,0:T(8,128)}, u32[]{:S(2)}, u32[]{:S(2)}) collective-permute-start(f32[256,256]{1,0:T(8,128)} %get-tuple-element.10.refs_0_), channel_id=1, source_target_pairs={{0,56},{8,0},{16,8},{24,16},{32,24},{40,32},{48,40},{56,48},{1,57}... | collective-permute-start | bytes 786440 | tf_op jit(solution)/shard_map/ppermute | solution.py:32
  96.4 20.7 %collective-permute-start.25 = (f32[256,256]{1,0:T(8,128)S(1)}, f32[256,256]{1,0:T(8,128)}, u32[]{:S(2)}, u32[]{:S(2)}) collective-permute-start(f32[256,256]{1,0:T(8,128)S(1)} %get-tuple-element.9.refs_8_), channel_id=1, source_target_pairs={{0,8},{8,16},{16,24},{24,32},{32,40},{40,48},{48,56},{56,0},{1,9},... | collective-permute-start | bytes 786440 | tf_op jit(solution)/shard_map/ppermute | solution.py:32
  105.5 1.2 copy-start
  106.7 51.0 %all-to-all-start.1 = ((f32[16,48,512]{2,1,0:T(8,128)}), f32[16,48,512]{2,1,0:T(8,128)}, u32[]{:S(2)}, u32[]{:S(2)}) async-start(f32[16,48,512]{2,1,0:T(8,128)} %bitcast.24), calls=%async_computation.1 | async-start | bytes 3145728 | tf_op jit(solution)/shard_map/all_to_all | solution.py:135
  113.0 9.1 %collective-permute-start.19 = (f32[256,256]{1,0:T(8,128)}, f32[256,256]{1,0:T(8,128)S(1)}, u32[]{:S(2)}, u32[]{:S(2)}) collective-permute-start(f32[256,256]{1,0:T(8,128)} %get-tuple-element.10.refs_0_), channel_id=1, source_target_pairs={{0,8},{8,16},{16,24},{24,32},{32,40},{40,48},{48,56},{56,0},{1,9},... | collective-permute-start | bytes 786440 | tf_op jit(solution)/shard_map/ppermute | solution.py:32
  113.1 9.1 %collective-permute-start.22 = (f32[256,256]{1,0:T(8,128)S(1)}, f32[256,256]{1,0:T(8,128)S(1)}, u32[]{:S(2)}, u32[]{:S(2)}) collective-permute-start(f32[256,256]{1,0:T(8,128)S(1)} %get-tuple-element.9.refs_8_), channel_id=1, source_target_pairs={{0,56},{8,0},{16,8},{24,16},{32,24},{40,32},{48,40},{56,48},{1,57}... | collective-permute-start | bytes 786440 | tf_op jit(solution)/shard_map/ppermute | solution.py:32
  115.8 11.2 %collective-permute-start.16 = (f32[256,256]{1,0:T(8,128)}, f32[256,256]{1,0:T(8,128)S(1)}, u32[]{:S(2)}, u32[]{:S(2)}) collective-permute-start(f32[256,256]{1,0:T(8,128)} %collective-permute-done.15.refs_1_), channel_id=1, source_target_pairs={{0,56},{8,0},{16,8},{24,16},{32,24},{40,32},{48,40},{56,48},{1,57}... | collective-permute-start | bytes 786440 | tf_op jit(solution)/shard_map/ppermute | solution.py:32
  117.1 12.8 %collective-permute-start.26 = (f32[256,256]{1,0:T(8,128)}, f32[256,256]{1,0:T(8,128)S(1)}, u32[]{:S(2)}, u32[]{:S(2)}) collective-permute-start(f32[256,256]{1,0:T(8,128)} %collective-permute-done.25.refs_15_), channel_id=1, source_target_pairs={{0,8},{8,16},{16,24},{24,32},{32,40},{40,48},{48,56},{56,0},{1,9},... | collective-permute-start | bytes 786440 | tf_op jit(solution)/shard_map/ppermute | solution.py:32
  122.1 11.2 %collective-permute-start.20 = (f32[256,256]{1,0:T(8,128)S(1)}, f32[256,256]{1,0:T(8,128)S(1)}, u32[]{:S(2)}, u32[]{:S(2)}) collective-permute-start(f32[256,256]{1,0:T(8,128)S(1)} %collective-permute-done.19.refs_7_), channel_id=1, source_target_pairs={{0,8},{8,16},{16,24},{24,32},{32,40},{40,48},{48,56},{56,0},{1,9},... | collective-permute-start | bytes 786440 | tf_op jit(solution)/shard_map/ppermute | solution.py:32
  122.1 11.2 %collective-permute-start.23 = (f32[256,256]{1,0:T(8,128)S(1)}, f32[256,256]{1,0:T(8,128)S(1)}, u32[]{:S(2)}, u32[]{:S(2)}) collective-permute-start(f32[256,256]{1,0:T(8,128)S(1)} %collective-permute-done.22.refs_9_), channel_id=1, source_target_pairs={{0,56},{8,0},{16,8},{24,16},{32,24},{40,32},{48,40},{56,48},{1,57}... | collective-permute-start | bytes 786440 | tf_op jit(solution)/shard_map/ppermute | solution.py:32
  127.0 11.1 %collective-permute-start.17 = (f32[256,256]{1,0:T(8,128)S(1)}, f32[256,256]{1,0:T(8,128)S(1)}, u32[]{:S(2)}, u32[]{:S(2)}) collective-permute-start(f32[256,256]{1,0:T(8,128)S(1)} %collective-permute-done.16.refs_2_), channel_id=1, source_target_pairs={{0,56},{8,0},{16,8},{24,16},{32,24},{40,32},{48,40},{56,48},{1,57}... | collective-permute-start | bytes 786440 | tf_op jit(solution)/shard_map/ppermute | solution.py:32
  130.0 11.2 %collective-permute-start.27 = (f32[256,256]{1,0:T(8,128)S(1)}, f32[256,256]{1,0:T(8,128)S(1)}, u32[]{:S(2)}, u32[]{:S(2)}) collective-permute-start(f32[256,256]{1,0:T(8,128)S(1)} %collective-permute-done.26.refs_14_), channel_id=1, source_target_pairs={{0,8},{8,16},{16,24},{24,32},{32,40},{40,48},{48,56},{56,0},{1,9},... | collective-permute-start | bytes 786440 | tf_op jit(solution)/shard_map/ppermute | solution.py:32
  133.4 9.5 %collective-permute-start.21 = (f32[256,256]{1,0:T(8,128)S(1)}, f32[256,256]{1,0:T(8,128)S(1)}, u32[]{:S(2)}, u32[]{:S(2)}) collective-permute-start(f32[256,256]{1,0:T(8,128)S(1)} %collective-permute-done.20.refs_6_), channel_id=1, source_target_pairs={{0,8},{8,16},{16,24},{24,32},{32,40},{40,48},{48,56},{56,0},{1,9},... | collective-permute-start | bytes 786440 | tf_op jit(solution)/shard_map/ppermute | solution.py:32
  133.4 10.4 %collective-permute-start.24 = (f32[256,256]{1,0:T(8,128)S(1)}, f32[256,256]{1,0:T(8,128)S(1)}, u32[]{:S(2)}, u32[]{:S(2)}) collective-permute-start(f32[256,256]{1,0:T(8,128)S(1)} %collective-permute-done.23.refs_10_), channel_id=1, source_target_pairs={{0,56},{8,0},{16,8},{24,16},{32,24},{40,32},{48,40},{56,48},{1,57}... | collective-permute-start | bytes 786440 | tf_op jit(solution)/shard_map/ppermute | solution.py:32
  138.1 11.2 %collective-permute-start.18 = (f32[256,256]{1,0:T(8,128)S(1)}, f32[256,256]{1,0:T(8,128)S(1)}, u32[]{:S(2)}, u32[]{:S(2)}) collective-permute-start(f32[256,256]{1,0:T(8,128)S(1)} %collective-permute-done.17.refs_3_), channel_id=1, source_target_pairs={{0,56},{8,0},{16,8},{24,16},{32,24},{40,32},{48,40},{56,48},{1,57}... | collective-permute-start | bytes 786440 | tf_op jit(solution)/shard_map/ppermute | solution.py:32
  141.1 8.2 %collective-permute-start.28 = (f32[256,256]{1,0:T(8,128)S(1)}, f32[256,256]{1,0:T(8,128)S(1)}, u32[]{:S(2)}, u32[]{:S(2)}) collective-permute-start(f32[256,256]{1,0:T(8,128)S(1)} %collective-permute-done.27.refs_13_), channel_id=1, source_target_pairs={{0,8},{8,16},{16,24},{24,32},{32,40},{40,48},{48,56},{56,0},{1,9},... | collective-permute-start | bytes 786440 | tf_op jit(solution)/shard_map/ppermute | solution.py:32
  156.5 1.2 copy-start.1
  157.7 7.6 %copy-start.4 = (s32[48,2]{0,1:T(2,128)S(1)}, s32[48,2]{0,1:T(2,128)}, u32[]{:S(2)}) copy-start(s32[48,2]{0,1:T(2,128)} %param.7) | copy-start | bytes 1156
  157.7 7.6 %copy-start.3 = (f32[200]{0:T(256)S(1)}, f32[200]{0:T(256)}, u32[]{:S(2)}) copy-start(f32[200]{0:T(256)} %param.8) | copy-start | bytes 2404
  157.7 29.5 %all-to-all-start.2 = ((f32[16,48,512]{2,1,0:T(8,128)}), f32[16,48,512]{2,1,0:T(8,128)S(1)}, u32[]{:S(2)}, u32[]{:S(2)}) async-start(f32[16,48,512]{2,1,0:T(8,128)} %bitcast.25), calls=%async_computation.2 | async-start | bytes 3145728 | tf_op jit(solution)/shard_map/all_to_all | solution.py:135
  165.5 21.9 %copy-start.2 = (f32[2048]{0:T(1024)S(1)}, f32[2048]{0:T(1024)}, u32[]{:S(2)}) copy-start(f32[2048]{0:T(1024)} %param.9) | copy-start | bytes 24580

commit v2 on v1

v2 whole, which is shorter than its diff:
```python
import functools

import jax
import jax.numpy as jnp
from jax import lax
from jax.experimental import pallas as pl
from jax.experimental.pallas import tpu as pltpu
from jax.sharding import Mesh
from jax.sharding import PartitionSpec as P


AXES = ("xhi", "core", "z", "xlo", "y")
LAYERS = 8
RING = 8
CHAINS = (512, 256, 256)
AHEAD = (4, 3, 3)
STAGES = (
    (((0, 7, None),), ((7, 8, 0), (0, 8, None))),
    (((0, 5, None), (0, 5, None)), ((5, 7, 0), (5, 7, 1)), ((7, 8, 0), (7, 8, 1))),
)
GROUPS = ((0,), (1, 2))
ARRIVAL = (0, 1, 7, 2, 6, 3, 5, 4)
SMEM = pl.BlockSpec(memory_space=pltpu.SMEM)
ANY = pl.BlockSpec(memory_space=pl.ANY)
VMEM_LIMIT = 60 * 1024 * 1024


def energy_lookup(pair_list, occupied_energy):
    occ_index = jnp.arange(occupied_energy.shape[0], dtype=jnp.int32)
    occ_first = jnp.sum(
        jnp.where(pair_list[:, 0:1] == occ_index[None, :], occupied_energy[None, :], 0.0), axis=1
    )
    occ_second = jnp.sum(
        jnp.where(pair_list[:, 1:2] == occ_index[None, :], occupied_energy[None, :], 0.0), axis=1
    )
    return (occ_first, occ_second)


def shift(value, axis, step):
    count = lax.axis_size(axis)
    return lax.ppermute(value, axis, [(i, (i + step) % count) for i in range(count)])


def sort_kernel(z_ref, amp_ref, out_ref, held_ref, in_sem, out_sem):
    depth = out_ref.shape[2] // RING
    span = LAYERS * depth
    loads, stores = [], []
    for p, s in enumerate(ARRIVAL):
        source = pl.multiple_of(lax.rem(z_ref[0] + s, RING) * span, span)
        loads.append(
            pltpu.make_async_copy(
                amp_ref.at[:, pl.ds(source, span)], held_ref.at[:, pl.ds(p * span, span)], in_sem.at[p]
            )
        )
        loads[-1].start()
    for p in range(RING):
        loads[p].wait()
        for layer in range(LAYERS):
            stores.append(
                pltpu.make_async_copy(
                    held_ref.at[:, pl.ds(p * span + layer * depth, depth)],
                    out_ref.at[layer, :, pl.ds(p * depth, depth)],
                    out_sem.at[p * LAYERS + layer],
                )
            )
            stores[-1].start()
    for store in stores:
        store.wait()


def sort_amplitudes(amplitudes, z, depth):
    rows = amplitudes.shape[0]
    return pl.pallas_call(
        sort_kernel,
        in_specs=[SMEM, ANY],
        out_specs=ANY,
        out_shape=jax.ShapeDtypeStruct((LAYERS, rows, RING * depth), jnp.float32),
        scratch_shapes=[
            pltpu.VMEM(amplitudes.shape, jnp.float32),
            pltpu.SemaphoreType.DMA((RING,)),
            pltpu.SemaphoreType.DMA((RING * LAYERS,)),
        ],
        compiler_params=pltpu.CompilerParams(vmem_limit_bytes=VMEM_LIMIT),
        cost_estimate=pl.CostEstimate(flops=0, bytes_accessed=8 * amplitudes.size, transcendentals=0),
        name="sort",
    )(z, amplitudes)


def split(value):
    high = value.astype(jnp.bfloat16)
    low = (value - high.astype(jnp.float32)).astype(jnp.bfloat16)
    return high, low


def product_kernel(jobs, count, final, core_ref, *refs):
    lefts, refs = refs[: len(jobs)], refs[len(jobs) :]
    summed = any(job[2] is not None for job in jobs)
    acc_ref, refs = (refs[0], refs[1:]) if summed else (None, refs)
    blocks, refs = refs[:count], refs[count:]
    out_ref, block_ref, left_ref, sum_ref, high_ref, low_ref, block_sem, left_sem, sum_sem, out_sem = refs
    first = min(job[0] for job in jobs)
    end = max(job[1] for job in jobs)
    span = end - first
    chains = count // span
    depth = block_ref.shape[0] // span
    wide = block_ref.shape[1] // chains
    rows = sum_ref.shape[1]
    middle = first + (span + 1) // 2 if span > 3 else end
    segments = [(first, middle), (middle, end)] if middle < end else [(first, end)]

    def local(lo, hi):
        return slice((lo - first) * depth, (hi - first) * depth)

    block_copies, left_copies, acc_copies = {}, {}, {}
    for n, (lo, hi) in enumerate(segments):
        for p in range(lo, hi):
            for c in range(chains):
                target = block_ref.at[local(p, p + 1), c * wide : (c + 1) * wide]
                block_copies[p, c] = pltpu.make_async_copy(
                    blocks[c * span + p - first], target, block_sem.at[(p - first) * chains + c]
                )
                block_copies[p, c].start()
        for j, job in enumerate(jobs):
            a, b = max(lo, job[0]), min(hi, job[1])
            if a < b:
                left_copies[n, j] = pltpu.make_async_copy(
                    lefts[j].at[:, a * depth : b * depth], left_ref.at[j, :, local(a, b)], left_sem.at[n, j]
                )
                left_copies[n, j].start()
                if job[2] is not None and j not in acc_copies:
                    acc_copies[j] = pltpu.make_async_copy(acc_ref.at[job[2]], sum_ref.at[j], sum_sem.at[j])
                    acc_copies[j].start()
    dot = functools.partial(jnp.dot, preferred_element_type=jnp.float32)
    begun = set()
    copies = []
    for n, (lo, hi) in enumerate(segments):
        for p in range(lo, hi):
            for c in range(chains):
                block_copies[p, c].wait()
        high, low = split(block_ref[local(lo, hi), :])
        high_ref[local(lo, hi), :] = high
        low_ref[local(lo, hi), :] = low
        for j in sorted(range(len(jobs)), key=lambda j: jobs[j][1] - jobs[j][0]):
            a, b = max(lo, jobs[j][0]), min(hi, jobs[j][1])
            if a >= b:
                continue
            left_copies[n, j].wait()
            high, low = split(left_ref[j, :, local(a, b)])
            value = (
                dot(high, low_ref[local(a, b), :])
                + dot(low, high_ref[local(a, b), :])
                + dot(high, high_ref[local(a, b), :])
            )
            if j in begun:
                sum_ref[j] += value
            elif jobs[j][2] is not None:
                acc_copies[j].wait()
                sum_ref[j] += value
            else:
                sum_ref[j] = value
            begun.add(j)
            if b == jobs[j][1]:
                if final:
                    core = core_ref[0]
                    start = pl.multiple_of((core if j == 0 else 1 - core) * rows, rows)
                    target = out_ref.at[pl.ds(start, rows)]
                else:
                    target = out_ref.at[j]
                copies.append(pltpu.make_async_copy(sum_ref.at[j], target, out_sem.at[j]))
                copies[-1].start()
    for copy in copies:
        copy.wait()


def product(core, lefts, jobs, acc, blocks, width, depth, final):
    rows = lefts[0].shape[0]
    span = max(job[1] for job in jobs) - min(job[0] for job in jobs)
    accs = [] if acc is None else [acc]
    shape = (2 * rows, width) if final else (len(jobs), rows, width)
    work = sum(job[1] - job[0] for job in jobs)
    return pl.pallas_call(
        functools.partial(product_kernel, jobs, len(blocks), final),
        in_specs=[SMEM] + [ANY] * (len(lefts) + len(accs) + len(blocks)),
        out_specs=ANY,
        out_shape=jax.ShapeDtypeStruct(shape, jnp.float32),
        scratch_shapes=[
            pltpu.VMEM((span * depth, width), jnp.float32),
            pltpu.VMEM((len(jobs), rows, span * depth), jnp.float32),
            pltpu.VMEM((len(jobs), rows, width), jnp.float32),
            pltpu.VMEM((span * depth, width), jnp.bfloat16),
            pltpu.VMEM((span * depth, width), jnp.bfloat16),
            pltpu.SemaphoreType.DMA((len(blocks),)),
            pltpu.SemaphoreType.DMA((2, len(jobs))),
            pltpu.SemaphoreType.DMA((len(jobs),)),
            pltpu.SemaphoreType.DMA((len(jobs),)),
        ],
        compiler_params=pltpu.CompilerParams(vmem_limit_bytes=VMEM_LIMIT),
        cost_estimate=pl.CostEstimate(
            flops=6 * work * rows * depth * width, bytes_accessed=4 * work * rows * depth, transcendentals=0
        ),
    )(core, *lefts, *accs, *blocks)


def body(amplitudes, integrals, pair_list, occupied_energy, virtual_energy):
    rows = amplitudes.shape[0]
    depth, cols = integrals.shape
    core = lax.axis_index("core")
    z = lax.axis_index("z")
    half = cols // 2
    chains = []
    start = 0
    for n, width in enumerate(CHAINS):
        block = lax.dynamic_slice(integrals, (0, core * half + start), (depth, width))
        plus = [block]
        minus = [block]
        ahead = AHEAD[n]
        for _ in range(1, ahead + 1):
            plus.append(shift(plus[-1], "z", -1))
        for _ in range(1, RING - ahead):
            minus.append(shift(minus[-1], "z", 1))
        ring = plus + minus[:0:-1]
        chains.append([ring[s] for s in ARRIVAL])
        start += width
    send = sort_amplitudes(amplitudes, z[None], depth)
    got = lax.all_to_all(send, ("xlo", "y"), split_axis=0, concat_axis=0, tiled=True)
    own = got.reshape(LAYERS * rows, RING * depth)
    other = lax.ppermute(own, "core", [(0, 1), (1, 0)])
    sums = []
    for g, group in enumerate(GROUPS):
        width = sum(CHAINS[n] for n in group)

        def part(lo, hi):
            return [chains[n][p] for n in group for p in range(lo, hi)]

        acc = None
        for n, jobs in enumerate(STAGES[g]):
            final = n == len(STAGES[g]) - 1
            span = (min(job[0] for job in jobs), max(job[1] for job in jobs))
            acc = product(core[None], [own, other][: len(jobs)], jobs, acc, part(*span), width, depth, final)
        partial = acc
        back = lax.all_to_all(
            partial.reshape(2 * LAYERS, rows, width), ("core", "xlo", "y"),
            split_axis=0, concat_axis=0, tiled=True,
        )
        sums.append(jnp.sum(back.reshape(2, LAYERS, rows, width), axis=1))
    ladder = jnp.concatenate([s[c] for c in range(2) for s in sums], axis=1)
    occ_first, occ_second = energy_lookup(pair_list, occupied_energy)
    denominator = virtual_energy[None, :] - occ_first[:, None] - occ_second[:, None]
    return ladder / denominator


def solution(mesh):
    fine = Mesh(mesh.devices.reshape(2, 2, 8, 2, 4), AXES)
    rows = P(AXES, None)
    in_specs = (rows, P(("z", "xlo", "y"), None), rows, P(), P())

    return jax.shard_map(body, mesh=fine, in_specs=in_specs, out_specs=rows, check_vma=False)
```

time: 189 us -> 206 us (1.090)
  waiting for transfers between devices: 59.8 us -> 78.8 us
  starting transfers between devices: 57.8 us -> 45.7 us
  Pallas kernels: 20.3 us -> 30.8 us
    ppermute x28 -> x21, waiting for transfers between devices: 39.7 us -> 57.3 us  [shift(): lax.ppermute(value, axis, [(i, (i + step) % count) for i in range(count)])]
    ppermute x28 -> x21, starting transfers between devices: 41.5 us -> 29.3 us  [shift(): lax.ppermute(value, axis, [(i, (i + step) % count) for i in range(count)])]
    pallas_call x3 -> x6, Pallas kernels: 20.3 us -> 30.8 us  [the longest x5 27.5 us: product(): pl.pallas_call(functools.partial(product_kernel, jobs, len(blocks), final...]
  transfers between devices with their start and end apart: 31 -> 24, of which waited for: 17 -> 11; matrix products, arithmetic and copies ran while one was open for 2% -> 1% of each run, Pallas kernels for 7% -> 10%
where the time goes in v2:
time: 206 us
  waiting for transfers between devices  78.8 us (38%)
  starting transfers between devices  45.7 us (22%)
  blocking collectives  43.1 us (21%)
  Pallas kernels  30.8 us (15%)
  local copies, waits for them, and re-layouts  5.85 us (3%)
    ppermute x21, waiting for transfers between devices, shift(): lax.ppermute(value, axis, [(i, (i + step) % count) for i in range(count)])  57.3 us
    all_to_all x1, blocking collectives, body(): lax.all_to_all(send, ('xlo', 'y'), split_axis=0, concat_axis=0, tiled=True)  43.1 us
    ppermute x21, starting transfers between devices, shift(): lax.ppermute(value, axis, [(i, (i + step) % count) for i in range(count)])  29.3 us
    pallas_call x5, Pallas kernels, product(): pl.pallas_call(functools.partial(product_kernel, jobs, len(blocks), final...  27.5 us
    all_to_all x2, waiting for transfers between devices, body(): lax.all_to_all(partial.reshape(2 * LAYERS, rows, width), ('core', 'xlo',...  21.5 us
    all_to_all x2, starting transfers between devices, body(): lax.all_to_all(partial.reshape(2 * LAYERS, rows, width), ('core', 'xlo',...  14 us
  transfers between devices with their start and end apart: 24, of which 11 were waited for; matrix products, arithmetic and copies ran while one was open for 1% of the time, Pallas kernels for 10%

profile of v2, /device:TPU:1, one launch (start us, length us, event | category | flops | bytes accessed | tf_op | source)
XLA Modules:
  0.0 205.9 jit_solution(8255594481766079609)
XLA Ops:
  0.0 3.3 %sort.1 = f32[8,48,2048]{2,1,0:T(8,128)} custom-call(s32[1]{0:T(128)} %bitcast.1.z_ref, f32[48,16384]{1,0:T(8,128)} %amp_ref.1), custom_call_target="tpu_custom_call" | custom-call | bytes 6291456 | tf_op jit(solution)/shard_map/sort/pallas_call | solution.py:73
  3.3 43.1 %all_to_all.15 = f32[8,48,2048]{2,1,0:T(8,128)S(1)} all-to-all(f32[8,48,2048]{2,1,0:T(8,128)} %sort.1), channel_id=1, replica_groups=mesh['xhi'=2,'core'=2,'z'=8,'xlo'=2,'y'=4] {'xlo','y'}, dimensions={0} | all-to-all | bytes 6291456 | tf_op jit(solution)/shard_map/all_to_all | solution.py:225
  46.4 2.4 %collective-permute-start = (f32[384,2048]{1,0:T(8,128)S(1)}, f32[384,2048]{1,0:T(8,128)}, u32[]{:S(2)}, u32[]{:S(2)}) collective-permute-start(f32[384,2048]{1,0:T(8,128)S(1)} %bitcast.21), channel_id=1, source_target_pairs={{0,64},{64,0},{1,65},{65,1},{2,66},{66,2},{3,67},{67,3},{4,68},{68... | collective-permute-start | bytes 9437192 | tf_op jit(solution)/shard_map/ppermute | solution.py:227
  48.8 1.1 constant_dynamic-slice_fusion.2.refs_1_.refs_3_
  49.9 5.7 %collective-permute-start.1 = (f32[256,512]{1,0:T(8,128)S(1)}, f32[256,512]{1,0:T(8,128)S(1)}, u32[]{:S(2)}, u32[]{:S(2)}) collective-permute-start(f32[256,512]{1,0:T(8,128)S(1)} %constant_dynamic-slice_fusion.2.refs_1_.refs_3_), channel_id=1, source_target_pairs={{0,56},{8,0},{16,8},{24,16},{32,24},{40,32},{48,40},{56,48},{1,57}... | collective-permute-start | bytes 1572872 | tf_op jit(solution)/shard_map/ppermute | solution.py:41
  55.5 0.0 collective-permute-start.2
  55.5 10.9 %collective-permute-done.1.refs_2_.refs_4_ = f32[256,512]{1,0:T(8,128)S(1)} collective-permute-done((f32[256,512]{1,0:T(8,128)S(1)}, f32[256,512]{1,0:T(8,128)S(1)}, u32[]{:S(2)}, u32[]{:S(2)}) %collective-permute-start.1) | collective-permute-done | bytes 524320 | tf_op jit(solution)/shard_map/ppermute | solution.py:41
  66.4 3.4 %collective-permute-start.3 = (f32[256,512]{1,0:T(8,128)S(1)}, f32[256,512]{1,0:T(8,128)S(1)}, u32[]{:S(2)}, u32[]{:S(2)}) collective-permute-start(f32[256,512]{1,0:T(8,128)S(1)} %collective-permute-done.1.refs_2_.refs_4_), channel_id=1, source_target_pairs={{0,56},{8,0},{16,8},{24,16},{32,24},{40,32},{48,40},{56,48},{1,57}... | collective-permute-start | bytes 1572872 | tf_op jit(solution)/shard_map/ppermute | solution.py:41
  69.8 0.0 collective-permute-done.2.refs_3_.refs_5_
  69.8 0.1 collective-permute-start.4
  69.9 9.9 %collective-permute-done.3.refs_4_.refs_6_ = f32[256,512]{1,0:T(8,128)S(1)} collective-permute-done((f32[256,512]{1,0:T(8,128)S(1)}, f32[256,512]{1,0:T(8,128)S(1)}, u32[]{:S(2)}, u32[]{:S(2)}) %collective-permute-start.3) | collective-permute-done | bytes 524320 | tf_op jit(solution)/shard_map/ppermute | solution.py:41
  79.9 3.4 %collective-permute-start.5 = (f32[256,512]{1,0:T(8,128)S(1)}, f32[256,512]{1,0:T(8,128)}, u32[]{:S(2)}, u32[]{:S(2)}) collective-permute-start(f32[256,512]{1,0:T(8,128)S(1)} %collective-permute-done.3.refs_4_.refs_6_), channel_id=1, source_target_pairs={{0,56},{8,0},{16,8},{24,16},{32,24},{40,32},{48,40},{56,48},{1,57}... | collective-permute-start | bytes 1572872 | tf_op jit(solution)/shard_map/ppermute | solution.py:41
  83.3 0.0 collective-permute-done.4.refs_5_.refs_7_
  83.3 0.1 collective-permute-start.6
  83.4 9.1 %collective-permute-done.5.refs_6_.refs_8_ = f32[256,512]{1,0:T(8,128)} collective-permute-done((f32[256,512]{1,0:T(8,128)S(1)}, f32[256,512]{1,0:T(8,128)}, u32[]{:S(2)}, u32[]{:S(2)}) %collective-permute-start.5) | collective-permute-done | bytes 524320 | tf_op jit(solution)/shard_map/ppermute | solution.py:41
  92.5 3.5 %collective-permute-start.7 = (f32[256,512]{1,0:T(8,128)}, f32[256,512]{1,0:T(8,128)}, u32[]{:S(2)}, u32[]{:S(2)}) collective-permute-start(f32[256,512]{1,0:T(8,128)} %collective-permute-done.5.refs_6_.refs_8_), channel_id=1, source_target_pairs={{0,56},{8,0},{16,8},{24,16},{32,24},{40,32},{48,40},{56,48},{1,57}... | collective-permute-start | bytes 1572872 | tf_op jit(solution)/shard_map/ppermute | solution.py:41
  96.0 0.8 copy-done.6
  96.8 5.9 %shard_map.55.refs_2_ = f32[1,384,512]{2,1,0:T(8,128)} custom-call(s32[1]{0:T(128)} %bitcast.core_ref, f32[384,2048]{1,0:T(8,128)} %bitcast.22, f32[256,512]{1,0:T(8,128)} %copy-done.1, f32[256,512]{1,0:T(8,128)} %copy-done.2, f32[256,512]{1,0:T(8,128)} %copy-done.3, f32[256,512]{1,0:T(8,128)} %copy-done.4, f32[256,512]{1,0:T(8,128)} %copy-done.5, ...), custom_call_target="tpu_custom_call" | custom-call | flops 2113929216 | bytes 2752512 | tf_op jit(solution)/shard_map/pallas_call | solution.py:181
  102.7 1.9 collective-permute-done.7.refs_10_
  104.6 0.0 collective-permute-done.refs_1_
  104.6 6.9 %shard_map.56 = f32[768,512]{1,0:T(8,128)} custom-call(s32[1]{0:T(128)} %bitcast.core_ref, f32[384,2048]{1,0:T(8,128)} %bitcast.23, f32[384,2048]{1,0:T(8,128)} %collective-permute-done.refs_1_, f32[1,384,512]{2,1,0:T(8,128)} %shard_map.55.refs_2_, f32[256,512]{1,0:T(8,128)} %copy-done.1, f32[256,512]{1,0:T(8,128)} %copy-done.2, f32[256,512]{1,0:T(8,128)} %copy-done.3, ...), custom_call_target="tpu_custom_call" | custom-call | flops 2717908992 | bytes 3538944 | tf_op jit(solution)/shard_map/pallas_call | solution.py:181
  111.6 7.4 %all-to-all-start.1 = ((f32[16,48,512]{2,1,0:T(8,128)}), f32[16,48,512]{2,1,0:T(8,128)S(1)}, u32[]{:S(2)}, u32[]{:S(2)}) async-start(f32[16,48,512]{2,1,0:T(8,128)} %bitcast.27), calls=%async_computation.1 | async-start | bytes 3145728 | tf_op jit(solution)/shard_map/all_to_all | solution.py:241
  119.0 1.1 constant_dynamic-slice_fusion
  120.1 0.0 copy-start.8
  120.1 0.3 collective-permute-start.9
  120.4 0.8 collective-permute-start.13
  121.1 2.8 %collective-permute-start.8 = (f32[256,256]{1,0:T(8,128)S(1)}, f32[256,256]{1,0:T(8,128)S(1)}, u32[]{:S(2)}, u32[]{:S(2)}) collective-permute-start(f32[256,256]{1,0:T(8,128)S(1)} %get-tuple-element.8.refs_2_), channel_id=1, source_target_pairs={{0,56},{8,0},{16,8},{24,16},{32,24},{40,32},{48,40},{56,48},{1,57}... | collective-permute-start | bytes 786440 | tf_op jit(solution)/shard_map/ppermute | solution.py:41
  123.9 1.4 collective-permute-start.12
  125.3 4.9 %collective-permute-done.9.refs_4_ = f32[256,256]{1,0:T(8,128)S(1)} collective-permute-done((f32[256,256]{1,0:T(8,128)S(1)}, f32[256,256]{1,0:T(8,128)S(1)}, u32[]{:S(2)}, u32[]{:S(2)}) %collective-permute-start.9) | collective-permute-done | bytes 262176 | tf_op jit(solution)/shard_map/ppermute | solution.py:41
  130.3 5.6 %collective-permute-done.13.refs_9_ = f32[256,256]{1,0:T(8,128)S(1)} collective-permute-done((f32[256,256]{1,0:T(8,128)S(1)}, f32[256,256]{1,0:T(8,128)S(1)}, u32[]{:S(2)}, u32[]{:S(2)}) %collective-permute-start.13) | collective-permute-done | bytes 262176 | tf_op jit(solution)/shard_map/ppermute | solution.py:41
  135.9 0.0 collective-permute-start.15
  135.9 0.0 collective-permute-done.8.refs_3_
  135.9 2.7 %collective-permute-start.10 = (f32[256,256]{1,0:T(8,128)S(1)}, f32[256,256]{1,0:T(8,128)}, u32[]{:S(2)}, u32[]{:S(2)}) collective-permute-start(f32[256,256]{1,0:T(8,128)S(1)} %collective-permute-done.8.refs_3_), channel_id=1, source_target_pairs={{0,56},{8,0},{16,8},{24,16},{32,24},{40,32},{48,40},{56,48},{1,57}... | collective-permute-start | bytes 786440 | tf_op jit(solution)/shard_map/ppermute | solution.py:41
  138.5 0.0 collective-permute-done.12.refs_8_
  138.6 0.1 collective-permute-start.14
  138.7 2.8 %collective-permute-done.11.refs_6_ = f32[256,256]{1,0:T(8,128)S(1)} collective-permute-done((f32[256,256]{1,0:T(8,128)S(1)}, f32[256,256]{1,0:T(8,128)S(1)}, u32[]{:S(2)}, u32[]{:S(2)}) %collective-permute-start.11) | collective-permute-done | bytes 262176 | tf_op jit(solution)/shard_map/ppermute | solution.py:41
  141.5 5.6 %collective-permute-done.15.refs_11_ = f32[256,256]{1,0:T(8,128)S(1)} collective-permute-done((f32[256,256]{1,0:T(8,128)S(1)}, f32[256,256]{1,0:T(8,128)S(1)}, u32[]{:S(2)}, u32[]{:S(2)}) %collective-permute-start.15) | collective-permute-done | bytes 262176 | tf_op jit(solution)/shard_map/ppermute | solution.py:41
  147.1 2.7 %collective-permute-start.16 = (f32[256,256]{1,0:T(8,128)}, f32[256,256]{1,0:T(8,128)S(1)}, u32[]{:S(2)}, u32[]{:S(2)}) collective-permute-start(f32[256,256]{1,0:T(8,128)} %collective-permute-done.10.refs_5_), channel_id=1, source_target_pairs={{0,56},{8,0},{16,8},{24,16},{32,24},{40,32},{48,40},{56,48},{1,57}... | collective-permute-start | bytes 786440 | tf_op jit(solution)/shard_map/ppermute | solution.py:41
  149.8 2.2 %collective-permute-start.18 = (f32[256,256]{1,0:T(8,128)}, f32[256,256]{1,0:T(8,128)S(1)}, u32[]{:S(2)}, u32[]{:S(2)}) collective-permute-start(f32[256,256]{1,0:T(8,128)} %collective-permute-done.14.refs_10_), channel_id=1, source_target_pairs={{0,56},{8,0},{16,8},{24,16},{32,24},{40,32},{48,40},{56,48},{1,57}... | collective-permute-start | bytes 786440 | tf_op jit(solution)/shard_map/ppermute | solution.py:41
  151.9 0.8 collective-permute-done.17.refs_4_
  152.7 0.0 collective-permute-start.20
  152.7 5.6 %collective-permute-done.19.refs_6_ = f32[256,256]{1,0:T(8,128)S(1)} collective-permute-done((f32[256,256]{1,0:T(8,128)S(1)}, f32[256,256]{1,0:T(8,128)S(1)}, u32[]{:S(2)}, u32[]{:S(2)}) %collective-permute-start.19) | collective-permute-done | bytes 262176 | tf_op jit(solution)/shard_map/ppermute | solution.py:41
  158.3 0.3 collective-permute-start.21
  158.7 6.6 %shard_map.57.refs_2_ = f32[2,384,512]{2,1,0:T(8,128)} custom-call(s32[1]{0:T(128)} %bitcast.core_ref, f32[384,2048]{1,0:T(8,128)} %bitcast.24, f32[384,2048]{1,0:T(8,128)} %collective-permute-done.refs_1_, f32[256,256]{1,0:T(8,128)} %copy-done.8, f32[256,256]{1,0:T(8,128)} %copy-done.20, f32[256,256]{1,0:T(8,128)} %copy-done.18, ...), custom_call_target="tpu_custom_call" | custom-call | flops 3019898880 | bytes 3932160 | tf_op jit(solution)/shard_map/pallas_call | solution.py:181
  165.3 0.0 collective-permute-done.16.refs_3_
  165.3 0.0 copy-start.13
  165.3 0.0 collective-permute-done.18.refs_5_
  165.3 0.7 copy-done.13
  166.0 0.7 copy-done.14
  166.7 4.5 %shard_map.58.refs_2_ = f32[2,384,512]{2,1,0:T(8,128)} custom-call(s32[1]{0:T(128)} %bitcast.core_ref, f32[384,2048]{1,0:T(8,128)} %bitcast.25, f32[384,2048]{1,0:T(8,128)} %collective-permute-done.refs_1_, f32[2,384,512]{2,1,0:T(8,128)} %shard_map.57.refs_2_, f32[256,256]{1,0:T(8,128)} %copy-done.13, f32[256,256]{1,0:T(8,128)} %copy-done.11, ...), custom_call_target="tpu_custom_call" | custom-call | flops 1207959552 | bytes 1572864 | tf_op jit(solution)/shard_map/pallas_call | solution.py:181
  171.2 0.0 collective-permute-done.20.refs_3_
  171.2 0.0 copy-start.9
  171.3 0.7 copy-done.9
  171.9 0.7 copy-done.10
  172.6 3.6 %shard_map.59 = f32[768,512]{1,0:T(8,128)} custom-call(s32[1]{0:T(128)} %bitcast.core_ref, f32[384,2048]{1,0:T(8,128)} %bitcast.26, f32[384,2048]{1,0:T(8,128)} %collective-permute-done.refs_1_, f32[2,384,512]{2,1,0:T(8,128)} %shard_map.58.refs_2_, f32[256,256]{1,0:T(8,128)} %copy-done.9, f32[256,256]{1,0:T(8,128)} %copy-done.10), custom_call_target="tpu_custom_call" | custom-call | flops 603979776 | bytes 786432 | tf_op jit(solution)/shard_map/pallas_call | solution.py:181
  176.3 0.0 copy-start.17
  176.3 0.0 copy-start.16
  176.3 6.6 %all-to-all-start.2 = ((f32[16,48,512]{2,1,0:T(8,128)}), f32[16,48,512]{2,1,0:T(8,128)S(1)}, u32[]{:S(2)}, u32[]{:S(2)}) async-start(f32[16,48,512]{2,1,0:T(8,128)} %bitcast.28), calls=%async_computation.2 | async-start | bytes 3145728 | tf_op jit(solution)/shard_map/all_to_all | solution.py:241
  182.9 0.2 select_reduce_fusion.1
  183.1 0.1 bitcast_reduce_fusion.1
  183.3 0.0 copy-start.15
  183.3 21.5 %all-to-all-done.2 = f32[16,48,512]{2,1,0:T(8,128)S(1)} async-done(((f32[16,48,512]{2,1,0:T(8,128)}), f32[16,48,512]{2,1,0:T(8,128)S(1)}, u32[]{:S(2)}, u32[]{:S(2)}) %all-to-all-start.2) | async-done | bytes 1572896 | tf_op jit(solution)/shard_map/all_to_all | solution.py:241
  204.8 0.1 bitcast_reduce_fusion
  205.0 0.9 maximum_divide_fusion
  (48 shorter events, 0.1 us)
Async XLA Ops:
  46.4 50.4 %copy-start = (f32[8,48,2048]{2,1,0:T(8,128)}, f32[8,48,2048]{2,1,0:T(8,128)S(1)}, u32[]{:S(2)}) copy-start(f32[8,48,2048]{2,1,0:T(8,128)S(1)} %all_to_all.15) | copy-start | bytes 9437188
  46.4 58.3 %collective-permute-start = (f32[384,2048]{1,0:T(8,128)S(1)}, f32[384,2048]{1,0:T(8,128)}, u32[]{:S(2)}, u32[]{:S(2)}) collective-permute-start(f32[384,2048]{1,0:T(8,128)S(1)} %bitcast.21), channel_id=1, source_target_pairs={{0,64},{64,0},{1,65},{65,1},{2,66},{66,2},{3,67},{67,3},{4,68},{68... | collective-permute-start | bytes 9437192 | tf_op jit(solution)/shard_map/ppermute | solution.py:227
  49.9 47.0 %copy-start.1 = (f32[256,512]{1,0:T(8,128)}, f32[256,512]{1,0:T(8,128)S(1)}, u32[]{:S(2)}) copy-start(f32[256,512]{1,0:T(8,128)S(1)} %constant_dynamic-slice_fusion.2.refs_1_.refs_3_) | copy-start | bytes 1572868
  49.9 16.6 %collective-permute-start.1 = (f32[256,512]{1,0:T(8,128)S(1)}, f32[256,512]{1,0:T(8,128)S(1)}, u32[]{:S(2)}, u32[]{:S(2)}) collective-permute-start(f32[256,512]{1,0:T(8,128)S(1)} %constant_dynamic-slice_fusion.2.refs_1_.refs_3_), channel_id=1, source_target_pairs={{0,56},{8,0},{16,8},{24,16},{32,24},{40,32},{48,40},{56,48},{1,57}... | collective-permute-start | bytes 1572872 | tf_op jit(solution)/shard_map/ppermute | solution.py:41
  55.5 14.3 %collective-permute-start.2 = (f32[256,512]{1,0:T(8,128)S(1)}, f32[256,512]{1,0:T(8,128)S(1)}, u32[]{:S(2)}, u32[]{:S(2)}) collective-permute-start(f32[256,512]{1,0:T(8,128)S(1)} %constant_dynamic-slice_fusion.2.refs_1_.refs_3_), channel_id=1, source_target_pairs={{0,8},{8,16},{16,24},{24,32},{32,40},{40,48},{48,56},{56,0},{1,9},... | collective-permute-start | bytes 1572872 | tf_op jit(solution)/shard_map/ppermute | solution.py:41
  66.4 3.4 %copy-start.2 = (f32[256,512]{1,0:T(8,128)}, f32[256,512]{1,0:T(8,128)S(1)}, u32[]{:S(2)}) copy-start(f32[256,512]{1,0:T(8,128)S(1)} %collective-permute-done.1.refs_2_.refs_4_) | copy-start | bytes 1572868
  66.4 13.5 %collective-permute-start.3 = (f32[256,512]{1,0:T(8,128)S(1)}, f32[256,512]{1,0:T(8,128)S(1)}, u32[]{:S(2)}, u32[]{:S(2)}) collective-permute-start(f32[256,512]{1,0:T(8,128)S(1)} %collective-permute-done.1.refs_2_.refs_4_), channel_id=1, source_target_pairs={{0,56},{8,0},{16,8},{24,16},{32,24},{40,32},{48,40},{56,48},{1,57}... | collective-permute-start | bytes 1572872 | tf_op jit(solution)/shard_map/ppermute | solution.py:41
  69.8 10.0 %copy-start.3 = (f32[256,512]{1,0:T(8,128)}, f32[256,512]{1,0:T(8,128)S(1)}, u32[]{:S(2)}) copy-start(f32[256,512]{1,0:T(8,128)S(1)} %collective-permute-done.2.refs_3_.refs_5_) | copy-start | bytes 1572868
  69.8 13.5 %collective-permute-start.4 = (f32[256,512]{1,0:T(8,128)S(1)}, f32[256,512]{1,0:T(8,128)S(1)}, u32[]{:S(2)}, u32[]{:S(2)}) collective-permute-start(f32[256,512]{1,0:T(8,128)S(1)} %collective-permute-done.2.refs_3_.refs_5_), channel_id=1, source_target_pairs={{0,8},{8,16},{16,24},{24,32},{32,40},{40,48},{48,56},{56,0},{1,9},... | collective-permute-start | bytes 1572872 | tf_op jit(solution)/shard_map/ppermute | solution.py:41
  79.9 3.4 %copy-start.4 = (f32[256,512]{1,0:T(8,128)}, f32[256,512]{1,0:T(8,128)S(1)}, u32[]{:S(2)}) copy-start(f32[256,512]{1,0:T(8,128)S(1)} %collective-permute-done.3.refs_4_.refs_6_) | copy-start | bytes 1572868
  79.9 12.6 %collective-permute-start.5 = (f32[256,512]{1,0:T(8,128)S(1)}, f32[256,512]{1,0:T(8,128)}, u32[]{:S(2)}, u32[]{:S(2)}) collective-permute-start(f32[256,512]{1,0:T(8,128)S(1)} %collective-permute-done.3.refs_4_.refs_6_), channel_id=1, source_target_pairs={{0,56},{8,0},{16,8},{24,16},{32,24},{40,32},{48,40},{56,48},{1,57}... | collective-permute-start | bytes 1572872 | tf_op jit(solution)/shard_map/ppermute | solution.py:41
  83.3 9.2 %copy-start.5 = (f32[256,512]{1,0:T(8,128)}, f32[256,512]{1,0:T(8,128)S(1)}, u32[]{:S(2)}) copy-start(f32[256,512]{1,0:T(8,128)S(1)} %collective-permute-done.4.refs_5_.refs_7_) | copy-start | bytes 1572868
  83.3 12.7 %collective-permute-start.6 = (f32[256,512]{1,0:T(8,128)S(1)}, f32[256,512]{1,0:T(8,128)S(1)}, u32[]{:S(2)}, u32[]{:S(2)}) collective-permute-start(f32[256,512]{1,0:T(8,128)S(1)} %collective-permute-done.4.refs_5_.refs_7_), channel_id=1, source_target_pairs={{0,8},{8,16},{16,24},{24,32},{32,40},{40,48},{48,56},{56,0},{1,9},... | collective-permute-start | bytes 1572872 | tf_op jit(solution)/shard_map/ppermute | solution.py:41
  92.5 12.2 %collective-permute-start.7 = (f32[256,512]{1,0:T(8,128)}, f32[256,512]{1,0:T(8,128)}, u32[]{:S(2)}, u32[]{:S(2)}) collective-permute-start(f32[256,512]{1,0:T(8,128)} %collective-permute-done.5.refs_6_.refs_8_), channel_id=1, source_target_pairs={{0,56},{8,0},{16,8},{24,16},{32,24},{40,32},{48,40},{56,48},{1,57}... | collective-permute-start | bytes 1572872 | tf_op jit(solution)/shard_map/ppermute | solution.py:41
  96.0 0.8 copy-start.6
  111.6 64.7 %all-to-all-start.1 = ((f32[16,48,512]{2,1,0:T(8,128)}), f32[16,48,512]{2,1,0:T(8,128)S(1)}, u32[]{:S(2)}, u32[]{:S(2)}) async-start(f32[16,48,512]{2,1,0:T(8,128)} %bitcast.27), calls=%async_computation.1 | async-start | bytes 3145728 | tf_op jit(solution)/shard_map/all_to_all | solution.py:241
  120.1 38.6 %copy-start.7 = (f32[256,256]{1,0:T(8,128)}, f32[256,256]{1,0:T(8,128)S(1)}, u32[]{:S(2)}) copy-start(f32[256,256]{1,0:T(8,128)S(1)} %get-tuple-element.7.refs_7_) | copy-start | bytes 786436
  120.1 38.6 %copy-start.8 = (f32[256,256]{1,0:T(8,128)}, f32[256,256]{1,0:T(8,128)S(1)}, u32[]{:S(2)}) copy-start(f32[256,256]{1,0:T(8,128)S(1)} %get-tuple-element.8.refs_2_) | copy-start | bytes 786436
  120.1 10.2 %collective-permute-start.9 = (f32[256,256]{1,0:T(8,128)S(1)}, f32[256,256]{1,0:T(8,128)S(1)}, u32[]{:S(2)}, u32[]{:S(2)}) collective-permute-start(f32[256,256]{1,0:T(8,128)S(1)} %get-tuple-element.8.refs_2_), channel_id=1, source_target_pairs={{0,8},{8,16},{16,24},{24,32},{32,40},{40,48},{48,56},{56,0},{1,9},... | collective-permute-start | bytes 786440 | tf_op jit(solution)/shard_map/ppermute | solution.py:41
  120.4 15.5 %collective-permute-start.13 = (f32[256,256]{1,0:T(8,128)S(1)}, f32[256,256]{1,0:T(8,128)S(1)}, u32[]{:S(2)}, u32[]{:S(2)}) collective-permute-start(f32[256,256]{1,0:T(8,128)S(1)} %get-tuple-element.7.refs_7_), channel_id=1, source_target_pairs={{0,8},{8,16},{16,24},{24,32},{32,40},{40,48},{48,56},{56,0},{1,9},... | collective-permute-start | bytes 786440 | tf_op jit(solution)/shard_map/ppermute | solution.py:41
  121.1 14.7 %collective-permute-start.8 = (f32[256,256]{1,0:T(8,128)S(1)}, f32[256,256]{1,0:T(8,128)S(1)}, u32[]{:S(2)}, u32[]{:S(2)}) collective-permute-start(f32[256,256]{1,0:T(8,128)S(1)} %get-tuple-element.8.refs_2_), channel_id=1, source_target_pairs={{0,56},{8,0},{16,8},{24,16},{32,24},{40,32},{48,40},{56,48},{1,57}... | collective-permute-start | bytes 786440 | tf_op jit(solution)/shard_map/ppermute | solution.py:41
  123.9 14.6 %collective-permute-start.12 = (f32[256,256]{1,0:T(8,128)S(1)}, f32[256,256]{1,0:T(8,128)S(1)}, u32[]{:S(2)}, u32[]{:S(2)}) collective-permute-start(f32[256,256]{1,0:T(8,128)S(1)} %get-tuple-element.7.refs_7_), channel_id=1, source_target_pairs={{0,56},{8,0},{16,8},{24,16},{32,24},{40,32},{48,40},{56,48},{1,57}... | collective-permute-start | bytes 786440 | tf_op jit(solution)/shard_map/ppermute | solution.py:41
  130.2 28.4 %copy-start.18 = (f32[256,256]{1,0:T(8,128)}, f32[256,256]{1,0:T(8,128)S(1)}, u32[]{:S(2)}) copy-start(f32[256,256]{1,0:T(8,128)S(1)} %collective-permute-done.9.refs_4_) | copy-start | bytes 786436
  130.2 11.2 %collective-permute-start.11 = (f32[256,256]{1,0:T(8,128)S(1)}, f32[256,256]{1,0:T(8,128)S(1)}, u32[]{:S(2)}, u32[]{:S(2)}) collective-permute-start(f32[256,256]{1,0:T(8,128)S(1)} %collective-permute-done.9.refs_4_), channel_id=1, source_target_pairs={{0,8},{8,16},{16,24},{24,32},{32,40},{40,48},{48,56},{56,0},{1,9},... | collective-permute-start | bytes 786440 | tf_op jit(solution)/shard_map/ppermute | solution.py:41
  135.9 16.1 %copy-start.19 = (f32[256,256]{1,0:T(8,128)}, f32[256,256]{1,0:T(8,128)S(1)}, u32[]{:S(2)}) copy-start(f32[256,256]{1,0:T(8,128)S(1)} %collective-permute-done.13.refs_9_) | copy-start | bytes 786436
  135.9 11.2 %collective-permute-start.15 = (f32[256,256]{1,0:T(8,128)S(1)}, f32[256,256]{1,0:T(8,128)S(1)}, u32[]{:S(2)}, u32[]{:S(2)}) collective-permute-start(f32[256,256]{1,0:T(8,128)S(1)} %collective-permute-done.13.refs_9_), channel_id=1, source_target_pairs={{0,8},{8,16},{16,24},{24,32},{32,40},{40,48},{48,56},{56,0},{1,9},... | collective-permute-start | bytes 786440 | tf_op jit(solution)/shard_map/ppermute | solution.py:41
  135.9 16.8 %copy-start.20 = (f32[256,256]{1,0:T(8,128)}, f32[256,256]{1,0:T(8,128)S(1)}, u32[]{:S(2)}) copy-start(f32[256,256]{1,0:T(8,128)S(1)} %collective-permute-done.8.refs_3_) | copy-start | bytes 786436
  135.9 11.2 %collective-permute-start.10 = (f32[256,256]{1,0:T(8,128)S(1)}, f32[256,256]{1,0:T(8,128)}, u32[]{:S(2)}, u32[]{:S(2)}) collective-permute-start(f32[256,256]{1,0:T(8,128)S(1)} %collective-permute-done.8.refs_3_), channel_id=1, source_target_pairs={{0,56},{8,0},{16,8},{24,16},{32,24},{40,32},{48,40},{56,48},{1,57}... | collective-permute-start | bytes 786440 | tf_op jit(solution)/shard_map/ppermute | solution.py:41
  138.6 11.2 %copy-start.21 = (f32[256,256]{1,0:T(8,128)}, f32[256,256]{1,0:T(8,128)S(1)}, u32[]{:S(2)}) copy-start(f32[256,256]{1,0:T(8,128)S(1)} %collective-permute-done.12.refs_8_) | copy-start | bytes 786436
  138.6 11.2 %collective-permute-start.14 = (f32[256,256]{1,0:T(8,128)S(1)}, f32[256,256]{1,0:T(8,128)}, u32[]{:S(2)}, u32[]{:S(2)}) collective-permute-start(f32[256,256]{1,0:T(8,128)S(1)} %collective-permute-done.12.refs_8_), channel_id=1, source_target_pairs={{0,56},{8,0},{16,8},{24,16},{32,24},{40,32},{48,40},{56,48},{1,57}... | collective-permute-start | bytes 786440 | tf_op jit(solution)/shard_map/ppermute | solution.py:41
  141.5 16.9 %copy-start.22 = (f32[256,256]{1,0:T(8,128)}, f32[256,256]{1,0:T(8,128)S(1)}, u32[]{:S(2)}) copy-start(f32[256,256]{1,0:T(8,128)S(1)} %collective-permute-done.11.refs_6_) | copy-start | bytes 786436
  141.5 11.2 %collective-permute-start.17 = (f32[256,256]{1,0:T(8,128)S(1)}, f32[256,256]{1,0:T(8,128)S(1)}, u32[]{:S(2)}, u32[]{:S(2)}) collective-permute-start(f32[256,256]{1,0:T(8,128)S(1)} %collective-permute-done.11.refs_6_), channel_id=1, source_target_pairs={{0,8},{8,16},{16,24},{24,32},{32,40},{40,48},{48,56},{56,0},{1,9},... | collective-permute-start | bytes 786440 | tf_op jit(solution)/shard_map/ppermute | solution.py:41
  147.1 11.2 %copy-start.23 = (f32[256,256]{1,0:T(8,128)}, f32[256,256]{1,0:T(8,128)S(1)}, u32[]{:S(2)}) copy-start(f32[256,256]{1,0:T(8,128)S(1)} %collective-permute-done.15.refs_11_) | copy-start | bytes 786436
  147.1 11.2 %collective-permute-start.19 = (f32[256,256]{1,0:T(8,128)S(1)}, f32[256,256]{1,0:T(8,128)S(1)}, u32[]{:S(2)}, u32[]{:S(2)}) collective-permute-start(f32[256,256]{1,0:T(8,128)S(1)} %collective-permute-done.15.refs_11_), channel_id=1, source_target_pairs={{0,8},{8,16},{16,24},{24,32},{32,40},{40,48},{48,56},{56,0},{1,9},... | collective-permute-start | bytes 786440 | tf_op jit(solution)/shard_map/ppermute | solution.py:41
  147.1 18.2 %collective-permute-start.16 = (f32[256,256]{1,0:T(8,128)}, f32[256,256]{1,0:T(8,128)S(1)}, u32[]{:S(2)}, u32[]{:S(2)}) collective-permute-start(f32[256,256]{1,0:T(8,128)} %collective-permute-done.10.refs_5_), channel_id=1, source_target_pairs={{0,56},{8,0},{16,8},{24,16},{32,24},{40,32},{48,40},{56,48},{1,57}... | collective-permute-start | bytes 786440 | tf_op jit(solution)/shard_map/ppermute | solution.py:41
  149.8 15.5 %collective-permute-start.18 = (f32[256,256]{1,0:T(8,128)}, f32[256,256]{1,0:T(8,128)S(1)}, u32[]{:S(2)}, u32[]{:S(2)}) collective-permute-start(f32[256,256]{1,0:T(8,128)} %collective-permute-done.14.refs_10_), channel_id=1, source_target_pairs={{0,56},{8,0},{16,8},{24,16},{32,24},{40,32},{48,40},{56,48},{1,57}... | collective-permute-start | bytes 786440 | tf_op jit(solution)/shard_map/ppermute | solution.py:41
  152.7 12.6 %copy-start.11 = (f32[256,256]{1,0:T(8,128)}, f32[256,256]{1,0:T(8,128)S(1)}, u32[]{:S(2)}) copy-start(f32[256,256]{1,0:T(8,128)S(1)} %collective-permute-done.17.refs_4_) | copy-start | bytes 786436
  152.7 18.5 %collective-permute-start.20 = (f32[256,256]{1,0:T(8,128)S(1)}, f32[256,256]{1,0:T(8,128)S(1)}, u32[]{:S(2)}, u32[]{:S(2)}) collective-permute-start(f32[256,256]{1,0:T(8,128)S(1)} %collective-permute-done.17.refs_4_), channel_id=1, source_target_pairs={{0,8},{8,16},{16,24},{24,32},{32,40},{40,48},{48,56},{56,0},{1,9},... | collective-permute-start | bytes 786440 | tf_op jit(solution)/shard_map/ppermute | solution.py:41
  158.3 6.9 %copy-start.12 = (f32[256,256]{1,0:T(8,128)}, f32[256,256]{1,0:T(8,128)S(1)}, u32[]{:S(2)}) copy-start(f32[256,256]{1,0:T(8,128)S(1)} %collective-permute-done.19.refs_6_) | copy-start | bytes 786436
  158.3 12.9 %collective-permute-start.21 = (f32[256,256]{1,0:T(8,128)S(1)}, f32[256,256]{1,0:T(8,128)S(1)}, u32[]{:S(2)}, u32[]{:S(2)}) collective-permute-start(f32[256,256]{1,0:T(8,128)S(1)} %collective-permute-done.19.refs_6_), channel_id=1, source_target_pairs={{0,8},{8,16},{16,24},{24,32},{32,40},{40,48},{48,56},{56,0},{1,9},... | collective-permute-start | bytes 786440 | tf_op jit(solution)/shard_map/ppermute | solution.py:41
  165.3 0.7 copy-start.13
  166.0 0.7 copy-start.14
  171.2 0.7 copy-start.9
  171.9 0.7 copy-start.10
  176.3 6.6 %copy-start.17 = (s32[48,2]{0,1:T(2,128)S(1)}, s32[48,2]{0,1:T(2,128)}, u32[]{:S(2)}) copy-start(s32[48,2]{0,1:T(2,128)} %param.7) | copy-start | bytes 1156
  176.3 6.6 %copy-start.16 = (f32[200]{0:T(256)S(1)}, f32[200]{0:T(256)}, u32[]{:S(2)}) copy-start(f32[200]{0:T(256)} %param.8) | copy-start | bytes 2404
  176.3 28.5 %all-to-all-start.2 = ((f32[16,48,512]{2,1,0:T(8,128)}), f32[16,48,512]{2,1,0:T(8,128)S(1)}, u32[]{:S(2)}, u32[]{:S(2)}) async-start(f32[16,48,512]{2,1,0:T(8,128)} %bitcast.28), calls=%async_computation.2 | async-start | bytes 3145728 | tf_op jit(solution)/shard_map/all_to_all | solution.py:241
  183.3 21.7 %copy-start.15 = (f32[2048]{0:T(1024)S(1)}, f32[2048]{0:T(1024)}, u32[]{:S(2)}) copy-start(f32[2048]{0:T(1024)} %param.9) | copy-start | bytes 24580

commit v3 on v2

--- a/solution.py
+++ b/solution.py
@@ -14,9 +14,10 @@
 RING = 8
 CHAINS = (512, 256, 256)
 AHEAD = (4, 3, 3)
+HALVED = ()
 STAGES = (
-    (((0, 7, None),), ((7, 8, 0), (0, 8, None))),
-    (((0, 5, None), (0, 5, None)), ((5, 7, 0), (5, 7, 1)), ((7, 8, 0), (7, 8, 1))),
+    (((0, 0, 7),), ((1, 0, 7),), ((0, 7, 8), (1, 7, 8))),
+    (((0, 0, 5), (1, 0, 5)), ((0, 5, 8), (1, 5, 8))),
 )
 GROUPS = ((0,), (1, 2))
 ARRIVAL = (0, 1, 7, 2, 6, 3, 5, 4)
@@ -94,19 +95,20 @@
 
 def product_kernel(jobs, count, final, core_ref, *refs):
     lefts, refs = refs[: len(jobs)], refs[len(jobs) :]
-    summed = any(job[2] is not None for job in jobs)
-    acc_ref, refs = (refs[0], refs[1:]) if summed else (None, refs)
-    blocks, refs = refs[:count], refs[count:]
-    out_ref, block_ref, left_ref, sum_ref, high_ref, low_ref, block_sem, left_sem, sum_sem, out_sem = refs
+    summed = [j for j, job in enumerate(jobs) if job[2]]
+    accs, refs = dict(zip(summed, refs)), refs[len(summed) :]
+    blocks, refs = refs[: sum(count)], refs[sum(count) :]
+    outs, refs = (refs[:1], refs[1:]) if final else (refs[: len(jobs)], refs[len(jobs) :])
+    block_ref, left_ref, sum_ref, high_ref, low_ref, block_sem, left_sem, sum_sem, out_sem = refs
     first = min(job[0] for job in jobs)
     end = max(job[1] for job in jobs)
     span = end - first
-    chains = count // span
+    chains = len(count) // span
     depth = block_ref.shape[0] // span
     wide = block_ref.shape[1] // chains
     rows = sum_ref.shape[1]
-    middle = first + (span + 1) // 2 if span > 3 else end
-    segments = [(first, middle), (middle, end)] if middle < end else [(first, end)]
+    cuts = [first] + [first + cut for cut in (1, 3) if cut < span - 1] + [end]
+    segments = list(zip(cuts, cuts[1:]))
 
     def local(lo, hi):
         return slice((lo - first) * depth, (hi - first) * depth)
@@ -115,11 +117,19 @@
     for n, (lo, hi) in enumerate(segments):
         for p in range(lo, hi):
             for c in range(chains):
-                target = block_ref.at[local(p, p + 1), c * wide : (c + 1) * wide]
-                block_copies[p, c] = pltpu.make_async_copy(
-                    blocks[c * span + p - first], target, block_sem.at[(p - first) * chains + c]
-                )
-                block_copies[p, c].start()
+                place = c * span + p - first
+                begin = sum(count[:place])
+                part = depth // count[place]
+                block_copies[p, c] = []
+                for k in range(count[place]):
+                    row = (p - first) * depth + k * part
+                    copy = pltpu.make_async_copy(
+                        blocks[begin + k],
+                        block_ref.at[row : row + part, c * wide : (c + 1) * wide],
+                        block_sem.at[begin + k],
+                    )
+                    copy.start()
+                    block_copies[p, c].append(copy)
         for j, job in enumerate(jobs):
             a, b = max(lo, job[0]), min(hi, job[1])
             if a < b:
@@ -127,8 +137,8 @@
                     lefts[j].at[:, a * depth : b * depth], left_ref.at[j, :, local(a, b)], left_sem.at[n, j]
                 )
                 left_copies[n, j].start()
-                if job[2] is not None and j not in acc_copies:
-                    acc_copies[j] = pltpu.make_async_copy(acc_ref.at[job[2]], sum_ref.at[j], sum_sem.at[j])
+                if j in accs and j not in acc_copies:
+                    acc_copies[j] = pltpu.make_async_copy(accs[j], sum_ref.at[j], sum_sem.at[j])
                     acc_copies[j].start()
     dot = functools.partial(jnp.dot, preferred_element_type=jnp.float32)
     begun = set()
@@ -136,7 +146,8 @@
     for n, (lo, hi) in enumerate(segments):
         for p in range(lo, hi):
             for c in range(chains):
-                block_copies[p, c].wait()
+                for copy in block_copies[p, c]:
+                    copy.wait()
         high, low = split(block_ref[local(lo, hi), :])
         high_ref[local(lo, hi), :] = high
         low_ref[local(lo, hi), :] = low
@@ -153,7 +164,7 @@
             )
             if j in begun:
                 sum_ref[j] += value
-            elif jobs[j][2] is not None:
+            elif j in accs:
                 acc_copies[j].wait()
                 sum_ref[j] += value
             else:
@@ -163,26 +174,27 @@
                 if final:
                     core = core_ref[0]
                     start = pl.multiple_of((core if j == 0 else 1 - core) * rows, rows)
-                    target = out_ref.at[pl.ds(start, rows)]
+                    target = outs[0].at[pl.ds(start, rows)]
                 else:
-                    target = out_ref.at[j]
+                    target = outs[j]
                 copies.append(pltpu.make_async_copy(sum_ref.at[j], target, out_sem.at[j]))
                 copies[-1].start()
     for copy in copies:
         copy.wait()
 
 
-def product(core, lefts, jobs, acc, blocks, width, depth, final):
+def product(core, lefts, jobs, accs, blocks, width, depth, final):
     rows = lefts[0].shape[0]
     span = max(job[1] for job in jobs) - min(job[0] for job in jobs)
-    accs = [] if acc is None else [acc]
-    shape = (2 * rows, width) if final else (len(jobs), rows, width)
+    shapes = [(2 * rows, width)] if final else [(rows, width)] * len(jobs)
     work = sum(job[1] - job[0] for job in jobs)
+    count = tuple(len(b) if isinstance(b, tuple) else 1 for b in blocks)
+    blocks = [x for b in blocks for x in (b if isinstance(b, tuple) else (b,))]
     return pl.pallas_call(
-        functools.partial(product_kernel, jobs, len(blocks), final),
+        functools.partial(product_kernel, jobs, count, final),
         in_specs=[SMEM] + [ANY] * (len(lefts) + len(accs) + len(blocks)),
-        out_specs=ANY,
-        out_shape=jax.ShapeDtypeStruct(shape, jnp.float32),
+        out_specs=[ANY] * len(shapes),
+        out_shape=[jax.ShapeDtypeStruct(shape, jnp.float32) for shape in shapes],
         scratch_shapes=[
             pltpu.VMEM((span * depth, width), jnp.float32),
             pltpu.VMEM((len(jobs), rows, span * depth), jnp.float32),
@@ -190,7 +202,7 @@
             pltpu.VMEM((span * depth, width), jnp.bfloat16),
             pltpu.VMEM((span * depth, width), jnp.bfloat16),
             pltpu.SemaphoreType.DMA((len(blocks),)),
-            pltpu.SemaphoreType.DMA((2, len(jobs))),
+            pltpu.SemaphoreType.DMA((3, len(jobs))),
             pltpu.SemaphoreType.DMA((len(jobs),)),
             pltpu.SemaphoreType.DMA((len(jobs),)),
         ],
@@ -216,9 +228,17 @@
         ahead = AHEAD[n]
         for _ in range(1, ahead + 1):
             plus.append(shift(plus[-1], "z", -1))
-        for _ in range(1, RING - ahead):
+        for _ in range(1, min(RING - ahead, 4)):
             minus.append(shift(minus[-1], "z", 1))
-        ring = plus + minus[:0:-1]
+        if ahead == 3 and n in HALVED:
+            near = plus[3][: depth // 2]
+            rest = minus[3][depth // 2 :]
+            far = (shift(near, "z", -1), shift(rest, "z", 1))
+        elif ahead == 3:
+            far = shift(minus[3], "z", 1)
+        else:
+            far = plus[4]
+        ring = plus[:4] + [far] + minus[:0:-1]
         chains.append([ring[s] for s in ARRIVAL])
         start += width
     send = sort_amplitudes(amplitudes, z[None], depth)
@@ -232,12 +252,22 @@
         def part(lo, hi):
             return [chains[n][p] for n in group for p in range(lo, hi)]
 
-        acc = None
-        for n, jobs in enumerate(STAGES[g]):
+        lefts = (own, other)
+        accs = [None, None]
+        for n, stage in enumerate(STAGES[g]):
             final = n == len(STAGES[g]) - 1
-            span = (min(job[0] for job in jobs), max(job[1] for job in jobs))
-            acc = product(core[None], [own, other][: len(jobs)], jobs, acc, part(*span), width, depth, final)
-        partial = acc
+            span = (min(job[1] for job in stage), max(job[2] for job in stage))
+            jobs = tuple((lo, hi, accs[k] is not None) for k, lo, hi in stage)
+            given = [accs[k] for k, _, _ in stage if accs[k] is not None]
+            results = product(
+                core[None], [lefts[k] for k, _, _ in stage], jobs, given, part(*span), width, depth,
+                final,
+            )
+            if final:
+                partial = results[0]
+            else:
+                for (k, _, _), result in zip(stage, results):
+                    accs[k] = result
         back = lax.all_to_all(
             partial.reshape(2 * LAYERS, rows, width), ("core", "xlo", "y"),
             split_axis=0, concat_axis=0, tiled=True,

time: 206 us -> 205 us (level)
  waiting for transfers between devices: 78.8 us -> 81.9 us
  starting transfers between devices: 45.7 us -> 43 us
    ppermute x21, waiting for transfers between devices: 57.3 us -> 60.4 us  [shift(): lax.ppermute(value, axis, [(i, (i + step) % count) for i in range(count)])]
  transfers between devices with their start and end apart: 24 -> 24, of which waited for: 11 -> 11; matrix products, arithmetic and copies ran while one was open for 1% -> 1% of each run, Pallas kernels for 10% -> 11%
where the time goes in v3:
time: 205 us; the launch traced here: 204 us
  waiting for transfers between devices  81.9 us (40%)
  blocking collectives  43.1 us (21%)
  starting transfers between devices  43 us (21%)
  Pallas kernels  29.8 us (15%)
  local copies, waits for them, and re-layouts  4.57 us (2%)
    ppermute x21, waiting for transfers between devices, shift(): lax.ppermute(value, axis, [(i, (i + step) % count) for i in range(count)])  60.4 us
    all_to_all x1, blocking collectives, body(): lax.all_to_all(send, ('xlo', 'y'), split_axis=0, concat_axis=0, tiled=True)  43.1 us
    ppermute x21, starting transfers between devices, shift(): lax.ppermute(value, axis, [(i, (i + step) % count) for i in range(count)])  27.4 us
    pallas_call x5, Pallas kernels, product(): pl.pallas_call(functools.partial(product_kernel, jobs, count, final), in_...  26.5 us
    all_to_all x2, waiting for transfers between devices, body(): lax.all_to_all(partial.reshape(2 * LAYERS, rows, width), ('core', 'xlo',...  21.5 us
    all_to_all x2, starting transfers between devices, body(): lax.all_to_all(partial.reshape(2 * LAYERS, rows, width), ('core', 'xlo',...  13.2 us
  transfers between devices with their start and end apart: 24, of which 11 were waited for; matrix products, arithmetic and copies ran while one was open for 1% of the time, Pallas kernels for 11%

profile of v3, /device:TPU:1, one launch (start us, length us, event | category | flops | bytes accessed | tf_op | source)
XLA Modules:
  0.0 204.1 jit_solution(1237888247776058033)
XLA Ops:
  0.0 3.4 %sort.1 = f32[8,48,2048]{2,1,0:T(8,128)} custom-call(s32[1]{0:T(128)} %bitcast.1.z_ref, f32[48,16384]{1,0:T(8,128)} %amp_ref.1), custom_call_target="tpu_custom_call" | custom-call | bytes 6291456 | tf_op jit(solution)/shard_map/sort/pallas_call | solution.py:74
  3.4 43.1 %all_to_all.15 = f32[8,48,2048]{2,1,0:T(8,128)S(1)} all-to-all(f32[8,48,2048]{2,1,0:T(8,128)} %sort.1), channel_id=1, replica_groups=mesh['xhi'=2,'core'=2,'z'=8,'xlo'=2,'y'=4] {'xlo','y'}, dimensions={0} | all-to-all | bytes 6291456 | tf_op jit(solution)/shard_map/all_to_all | solution.py:245
  46.4 2.4 %collective-permute-start = (f32[384,2048]{1,0:T(8,128)S(1)}, f32[384,2048]{1,0:T(8,128)}, u32[]{:S(2)}, u32[]{:S(2)}) collective-permute-start(f32[384,2048]{1,0:T(8,128)S(1)} %bitcast.21), channel_id=1, source_target_pairs={{0,64},{64,0},{1,65},{65,1},{2,66},{66,2},{3,67},{67,3},{4,68},{68... | collective-permute-start | bytes 9437192 | tf_op jit(solution)/shard_map/ppermute | solution.py:247
  48.8 1.1 constant_dynamic-slice_fusion.2.refs_1_
  49.9 5.7 %collective-permute-start.1 = (f32[256,512]{1,0:T(8,128)S(1)}, f32[256,512]{1,0:T(8,128)S(1)}, u32[]{:S(2)}, u32[]{:S(2)}) collective-permute-start(f32[256,512]{1,0:T(8,128)S(1)} %constant_dynamic-slice_fusion.2.refs_1_), channel_id=1, source_target_pairs={{0,56},{8,0},{16,8},{24,16},{32,24},{40,32},{48,40},{56,48},{1,57}... | collective-permute-start | bytes 1572872 | tf_op jit(solution)/shard_map/ppermute | solution.py:42
  55.6 0.0 collective-permute-start.2
  55.6 10.9 %collective-permute-done.1.refs_2_ = f32[256,512]{1,0:T(8,128)S(1)} collective-permute-done((f32[256,512]{1,0:T(8,128)S(1)}, f32[256,512]{1,0:T(8,128)S(1)}, u32[]{:S(2)}, u32[]{:S(2)}) %collective-permute-start.1) | collective-permute-done | bytes 524320 | tf_op jit(solution)/shard_map/ppermute | solution.py:42
  66.5 3.4 %collective-permute-start.3 = (f32[256,512]{1,0:T(8,128)S(1)}, f32[256,512]{1,0:T(8,128)S(1)}, u32[]{:S(2)}, u32[]{:S(2)}) collective-permute-start(f32[256,512]{1,0:T(8,128)S(1)} %collective-permute-done.1.refs_2_), channel_id=1, source_target_pairs={{0,56},{8,0},{16,8},{24,16},{32,24},{40,32},{48,40},{56,48},{1,57}... | collective-permute-start | bytes 1572872 | tf_op jit(solution)/shard_map/ppermute | solution.py:42
  69.9 0.0 collective-permute-done.2.refs_3_
  69.9 0.0 collective-permute-start.4
  69.9 10.0 %collective-permute-done.3.refs_4_ = f32[256,512]{1,0:T(8,128)S(1)} collective-permute-done((f32[256,512]{1,0:T(8,128)S(1)}, f32[256,512]{1,0:T(8,128)S(1)}, u32[]{:S(2)}, u32[]{:S(2)}) %collective-permute-start.3) | collective-permute-done | bytes 524320 | tf_op jit(solution)/shard_map/ppermute | solution.py:42
  79.9 3.4 %collective-permute-start.5 = (f32[256,512]{1,0:T(8,128)S(1)}, f32[256,512]{1,0:T(8,128)}, u32[]{:S(2)}, u32[]{:S(2)}) collective-permute-start(f32[256,512]{1,0:T(8,128)S(1)} %collective-permute-done.3.refs_4_), channel_id=1, source_target_pairs={{0,56},{8,0},{16,8},{24,16},{32,24},{40,32},{48,40},{56,48},{1,57}... | collective-permute-start | bytes 1572872 | tf_op jit(solution)/shard_map/ppermute | solution.py:42
  83.4 0.0 collective-permute-done.4.refs_5_
  83.4 0.0 collective-permute-start.6
  83.4 9.2 %collective-permute-done.5.refs_6_ = f32[256,512]{1,0:T(8,128)} collective-permute-done((f32[256,512]{1,0:T(8,128)S(1)}, f32[256,512]{1,0:T(8,128)}, u32[]{:S(2)}, u32[]{:S(2)}) %collective-permute-start.5) | collective-permute-done | bytes 524320 | tf_op jit(solution)/shard_map/ppermute | solution.py:42
  92.5 3.5 %collective-permute-start.7 = (f32[256,512]{1,0:T(8,128)}, f32[256,512]{1,0:T(8,128)S(1)}, u32[]{:S(2)}, u32[]{:S(2)}) collective-permute-start(f32[256,512]{1,0:T(8,128)} %collective-permute-done.5.refs_6_), channel_id=1, source_target_pairs={{0,56},{8,0},{16,8},{24,16},{32,24},{40,32},{48,40},{56,48},{1,57}... | collective-permute-start | bytes 1572872 | tf_op jit(solution)/shard_map/ppermute | solution.py:42
  96.1 0.0 collective-permute-done.6.refs_7_
  96.1 0.8 copy-done.18
  96.9 5.6 %shard_map.55.refs_2_ = f32[384,512]{1,0:T(8,128)} custom-call(s32[1]{0:T(128)} %bitcast.core_ref, f32[384,2048]{1,0:T(8,128)} %bitcast.22, f32[256,512]{1,0:T(8,128)} %copy-done.2, f32[256,512]{1,0:T(8,128)} %copy-done.14, f32[256,512]{1,0:T(8,128)} %copy-done.15, f32[256,512]{1,0:T(8,128)} %copy-done.16, f32[256,512]{1,0:T(8,128)} %copy-done.17, ...), custom_call_target="tpu_custom_call" | custom-call | flops 2113929216 | bytes 2752512 | tf_op jit(solution)/shard_map/pallas_call | solution.py:193
  102.6 0.0 collective-permute-done.refs_0_.refs_1_
  102.6 5.6 %shard_map.56.refs_3_ = f32[384,512]{1,0:T(8,128)} custom-call(s32[1]{0:T(128)} %bitcast.core_ref, f32[384,2048]{1,0:T(8,128)} %collective-permute-done.refs_0_.refs_1_, f32[256,512]{1,0:T(8,128)} %copy-done.2, f32[256,512]{1,0:T(8,128)} %copy-done.14, f32[256,512]{1,0:T(8,128)} %copy-done.15, f32[256,512]{1,0:T(8,128)} %copy-done.16, ...), custom_call_target="tpu_custom_call" | custom-call | flops 2113929216 | bytes 2752512 | tf_op jit(solution)/shard_map/pallas_call | solution.py:193
  108.1 0.0 collective-permute-done.7.refs_4_
  108.2 0.8 copy-done.1
  109.0 3.5 %shard_map.57 = f32[768,512]{1,0:T(8,128)} custom-call(s32[1]{0:T(128)} %bitcast.core_ref, f32[384,2048]{1,0:T(8,128)} %bitcast.23, f32[384,2048]{1,0:T(8,128)} %collective-permute-done.refs_0_.refs_1_, f32[384,512]{1,0:T(8,128)} %shard_map.55.refs_2_, f32[384,512]{1,0:T(8,128)} %shard_map.56.refs_3_, f32[256,512]{1,0:T(8,128)} %copy-done.1), custom_call_target="tpu_custom_call" | custom-call | flops 603979776 | bytes 786432 | tf_op jit(solution)/shard_map/pallas_call | solution.py:193
  112.5 6.8 %all-to-all-start.1 = ((f32[16,48,512]{2,1,0:T(8,128)}), f32[16,48,512]{2,1,0:T(8,128)S(1)}, u32[]{:S(2)}, u32[]{:S(2)}) async-start(f32[16,48,512]{2,1,0:T(8,128)} %bitcast.26), calls=%async_computation.1 | async-start | bytes 3145728 | tf_op jit(solution)/shard_map/all_to_all | solution.py:271
  119.4 1.1 constant_dynamic-slice_fusion
  120.4 0.0 copy-start.4
  120.4 0.3 collective-permute-start.9
  120.7 0.1 collective-permute-start.13
  120.8 2.7 %collective-permute-start.8 = (f32[256,256]{1,0:T(8,128)S(1)}, f32[256,256]{1,0:T(8,128)S(1)}, u32[]{:S(2)}, u32[]{:S(2)}) collective-permute-start(f32[256,256]{1,0:T(8,128)S(1)} %get-tuple-element.12.refs_2_), channel_id=1, source_target_pairs={{0,56},{8,0},{16,8},{24,16},{32,24},{40,32},{48,40},{56,48},{1,57}... | collective-permute-start | bytes 786440 | tf_op jit(solution)/shard_map/ppermute | solution.py:42
  123.5 1.4 collective-permute-start.12
  124.8 4.7 %collective-permute-done.9.refs_4_ = f32[256,256]{1,0:T(8,128)S(1)} collective-permute-done((f32[256,256]{1,0:T(8,128)S(1)}, f32[256,256]{1,0:T(8,128)S(1)}, u32[]{:S(2)}, u32[]{:S(2)}) %collective-permute-start.9) | collective-permute-done | bytes 262176 | tf_op jit(solution)/shard_map/ppermute | solution.py:42
  129.6 0.0 collective-permute-start.11
  129.6 5.6 %collective-permute-done.13.refs_9_ = f32[256,256]{1,0:T(8,128)S(1)} collective-permute-done((f32[256,256]{1,0:T(8,128)S(1)}, f32[256,256]{1,0:T(8,128)S(1)}, u32[]{:S(2)}, u32[]{:S(2)}) %collective-permute-start.13) | collective-permute-done | bytes 262176 | tf_op jit(solution)/shard_map/ppermute | solution.py:42
  135.2 0.0 collective-permute-start.15
  135.2 0.0 collective-permute-done.8.refs_3_
  135.2 2.7 %collective-permute-start.10 = (f32[256,256]{1,0:T(8,128)S(1)}, f32[256,256]{1,0:T(8,128)}, u32[]{:S(2)}, u32[]{:S(2)}) collective-permute-start(f32[256,256]{1,0:T(8,128)S(1)} %collective-permute-done.8.refs_3_), channel_id=1, source_target_pairs={{0,56},{8,0},{16,8},{24,16},{32,24},{40,32},{48,40},{56,48},{1,57}... | collective-permute-start | bytes 786440 | tf_op jit(solution)/shard_map/ppermute | solution.py:42
  137.9 0.0 collective-permute-done.12.refs_8_
  137.9 0.1 collective-permute-start.14
  138.0 2.8 %collective-permute-done.11.refs_6_ = f32[256,256]{1,0:T(8,128)S(1)} collective-permute-done((f32[256,256]{1,0:T(8,128)S(1)}, f32[256,256]{1,0:T(8,128)S(1)}, u32[]{:S(2)}, u32[]{:S(2)}) %collective-permute-start.11) | collective-permute-done | bytes 262176 | tf_op jit(solution)/shard_map/ppermute | solution.py:42
  140.8 5.6 %collective-permute-done.15.refs_11_ = f32[256,256]{1,0:T(8,128)S(1)} collective-permute-done((f32[256,256]{1,0:T(8,128)S(1)}, f32[256,256]{1,0:T(8,128)S(1)}, u32[]{:S(2)}, u32[]{:S(2)}) %collective-permute-start.15) | collective-permute-done | bytes 262176 | tf_op jit(solution)/shard_map/ppermute | solution.py:42
  146.4 0.0 collective-permute-start.20
  146.5 2.7 %collective-permute-start.16 = (f32[256,256]{1,0:T(8,128)}, f32[256,256]{1,0:T(8,128)S(1)}, u32[]{:S(2)}, u32[]{:S(2)}) collective-permute-start(f32[256,256]{1,0:T(8,128)} %collective-permute-done.10.refs_5_), channel_id=1, source_target_pairs={{0,56},{8,0},{16,8},{24,16},{32,24},{40,32},{48,40},{56,48},{1,57}... | collective-permute-start | bytes 786440 | tf_op jit(solution)/shard_map/ppermute | solution.py:42
  149.1 1.6 collective-permute-start.19
  150.7 1.3 collective-permute-done.17.refs_5_
  152.1 0.0 collective-permute-start.18
  152.1 5.6 %collective-permute-done.20.refs_8_ = f32[256,256]{1,0:T(8,128)S(1)} collective-permute-done((f32[256,256]{1,0:T(8,128)S(1)}, f32[256,256]{1,0:T(8,128)S(1)}, u32[]{:S(2)}, u32[]{:S(2)}) %collective-permute-start.20) | collective-permute-done | bytes 262176 | tf_op jit(solution)/shard_map/ppermute | solution.py:42
  157.7 0.0 collective-permute-start.21
  157.7 6.5 %shard_map.58 = (f32[384,512]{1,0:T(8,128)}, f32[384,512]{1,0:T(8,128)}) custom-call(s32[1]{0:T(128)} %bitcast.core_ref, f32[384,2048]{1,0:T(8,128)} %bitcast.24, f32[384,2048]{1,0:T(8,128)} %collective-permute-done.refs_0_.refs_1_, f32[256,256]{1,0:T(8,128)} %copy-done.4, f32[256,256]{1,0:T(8,128)} %copy-done.21, f32[256,256]{1,0:T(8,128)} %copy-done.19, ...), custom_call_target="tpu_custom_call" | custom-call | flops 3019898880 | bytes 3932160 | tf_op jit(solution)/shard_map/pallas_call | solution.py:193
  164.3 0.0 collective-permute-done.16.refs_4_
  164.3 0.0 copy-start.7
  164.3 0.0 collective-permute-done.18.refs_6_
  164.3 4.6 %collective-permute-done.21.refs_9_ = f32[256,256]{1,0:T(8,128)S(1)} collective-permute-done((f32[256,256]{1,0:T(8,128)S(1)}, f32[256,256]{1,0:T(8,128)S(1)}, u32[]{:S(2)}, u32[]{:S(2)}) %collective-permute-start.21) | collective-permute-done | bytes 262176 | tf_op jit(solution)/shard_map/ppermute | solution.py:42
  168.9 0.7 copy-done.10
  169.6 5.2 %shard_map.59 = f32[768,512]{1,0:T(8,128)} custom-call(s32[1]{0:T(128)} %bitcast.core_ref, f32[384,2048]{1,0:T(8,128)} %bitcast.25, f32[384,2048]{1,0:T(8,128)} %collective-permute-done.refs_0_.refs_1_, f32[384,512]{1,0:T(8,128)} %get-tuple-element.7.refs_2_, f32[384,512]{1,0:T(8,128)} %get-tuple-element.8.refs_3_, f32[256,256]{1,0:T(8,128)} %copy-done.7, ...), custom_call_target="tpu_custom_call" | custom-call | flops 1811939328 | bytes 2359296 | tf_op jit(solution)/shard_map/pallas_call | solution.py:193
  174.8 0.0 copy-start.13
  174.8 0.0 copy-start.12
  174.8 6.3 %all-to-all-start.2 = ((f32[16,48,512]{2,1,0:T(8,128)}), f32[16,48,512]{2,1,0:T(8,128)S(1)}, u32[]{:S(2)}, u32[]{:S(2)}) async-start(f32[16,48,512]{2,1,0:T(8,128)} %bitcast.27), calls=%async_computation.2 | async-start | bytes 3145728 | tf_op jit(solution)/shard_map/all_to_all | solution.py:271
  181.2 0.2 select_reduce_fusion.1
  181.4 0.0 copy-start.11
  181.4 0.1 bitcast_reduce_fusion.1
  181.6 21.5 %all-to-all-done.2 = f32[16,48,512]{2,1,0:T(8,128)S(1)} async-done(((f32[16,48,512]{2,1,0:T(8,128)}), f32[16,48,512]{2,1,0:T(8,128)S(1)}, u32[]{:S(2)}, u32[]{:S(2)}) %all-to-all-start.2) | async-done | bytes 1572896 | tf_op jit(solution)/shard_map/all_to_all | solution.py:271
  203.1 0.1 bitcast_reduce_fusion
  203.2 0.9 maximum_divide_fusion
  (50 shorter events, 0.1 us)
Async XLA Ops:
  46.4 50.5 %copy-start = (f32[8,48,2048]{2,1,0:T(8,128)}, f32[8,48,2048]{2,1,0:T(8,128)S(1)}, u32[]{:S(2)}) copy-start(f32[8,48,2048]{2,1,0:T(8,128)S(1)} %all_to_all.15) | copy-start | bytes 9437188
  46.4 56.1 %collective-permute-start = (f32[384,2048]{1,0:T(8,128)S(1)}, f32[384,2048]{1,0:T(8,128)}, u32[]{:S(2)}, u32[]{:S(2)}) collective-permute-start(f32[384,2048]{1,0:T(8,128)S(1)} %bitcast.21), channel_id=1, source_target_pairs={{0,64},{64,0},{1,65},{65,1},{2,66},{66,2},{3,67},{67,3},{4,68},{68... | collective-permute-start | bytes 9437192 | tf_op jit(solution)/shard_map/ppermute | solution.py:247
  49.9 33.4 %copy-start.2 = (f32[256,512]{1,0:T(8,128)}, f32[256,512]{1,0:T(8,128)S(1)}, u32[]{:S(2)}) copy-start(f32[256,512]{1,0:T(8,128)S(1)} %constant_dynamic-slice_fusion.2.refs_1_) | copy-start | bytes 1572868
  49.9 16.6 %collective-permute-start.1 = (f32[256,512]{1,0:T(8,128)S(1)}, f32[256,512]{1,0:T(8,128)S(1)}, u32[]{:S(2)}, u32[]{:S(2)}) collective-permute-start(f32[256,512]{1,0:T(8,128)S(1)} %constant_dynamic-slice_fusion.2.refs_1_), channel_id=1, source_target_pairs={{0,56},{8,0},{16,8},{24,16},{32,24},{40,32},{48,40},{56,48},{1,57}... | collective-permute-start | bytes 1572872 | tf_op jit(solution)/shard_map/ppermute | solution.py:42
  55.6 14.3 %collective-permute-start.2 = (f32[256,512]{1,0:T(8,128)S(1)}, f32[256,512]{1,0:T(8,128)S(1)}, u32[]{:S(2)}, u32[]{:S(2)}) collective-permute-start(f32[256,512]{1,0:T(8,128)S(1)} %constant_dynamic-slice_fusion.2.refs_1_), channel_id=1, source_target_pairs={{0,8},{8,16},{16,24},{24,32},{32,40},{40,48},{48,56},{56,0},{1,9},... | collective-permute-start | bytes 1572872 | tf_op jit(solution)/shard_map/ppermute | solution.py:42
  66.5 26.1 %copy-start.14 = (f32[256,512]{1,0:T(8,128)}, f32[256,512]{1,0:T(8,128)S(1)}, u32[]{:S(2)}) copy-start(f32[256,512]{1,0:T(8,128)S(1)} %collective-permute-done.1.refs_2_) | copy-start | bytes 1572868
  66.5 13.5 %collective-permute-start.3 = (f32[256,512]{1,0:T(8,128)S(1)}, f32[256,512]{1,0:T(8,128)S(1)}, u32[]{:S(2)}, u32[]{:S(2)}) collective-permute-start(f32[256,512]{1,0:T(8,128)S(1)} %collective-permute-done.1.refs_2_), channel_id=1, source_target_pairs={{0,56},{8,0},{16,8},{24,16},{32,24},{40,32},{48,40},{56,48},{1,57}... | collective-permute-start | bytes 1572872 | tf_op jit(solution)/shard_map/ppermute | solution.py:42
  69.9 26.2 %copy-start.15 = (f32[256,512]{1,0:T(8,128)}, f32[256,512]{1,0:T(8,128)S(1)}, u32[]{:S(2)}) copy-start(f32[256,512]{1,0:T(8,128)S(1)} %collective-permute-done.2.refs_3_) | copy-start | bytes 1572868
  69.9 13.5 %collective-permute-start.4 = (f32[256,512]{1,0:T(8,128)S(1)}, f32[256,512]{1,0:T(8,128)S(1)}, u32[]{:S(2)}, u32[]{:S(2)}) collective-permute-start(f32[256,512]{1,0:T(8,128)S(1)} %collective-permute-done.2.refs_3_), channel_id=1, source_target_pairs={{0,8},{8,16},{16,24},{24,32},{32,40},{40,48},{48,56},{56,0},{1,9},... | collective-permute-start | bytes 1572872 | tf_op jit(solution)/shard_map/ppermute | solution.py:42
  79.9 16.1 %copy-start.16 = (f32[256,512]{1,0:T(8,128)}, f32[256,512]{1,0:T(8,128)S(1)}, u32[]{:S(2)}) copy-start(f32[256,512]{1,0:T(8,128)S(1)} %collective-permute-done.3.refs_4_) | copy-start | bytes 1572868
  79.9 12.6 %collective-permute-start.5 = (f32[256,512]{1,0:T(8,128)S(1)}, f32[256,512]{1,0:T(8,128)}, u32[]{:S(2)}, u32[]{:S(2)}) collective-permute-start(f32[256,512]{1,0:T(8,128)S(1)} %collective-permute-done.3.refs_4_), channel_id=1, source_target_pairs={{0,56},{8,0},{16,8},{24,16},{32,24},{40,32},{48,40},{56,48},{1,57}... | collective-permute-start | bytes 1572872 | tf_op jit(solution)/shard_map/ppermute | solution.py:42
  83.4 12.7 %copy-start.17 = (f32[256,512]{1,0:T(8,128)}, f32[256,512]{1,0:T(8,128)S(1)}, u32[]{:S(2)}) copy-start(f32[256,512]{1,0:T(8,128)S(1)} %collective-permute-done.4.refs_5_) | copy-start | bytes 1572868
  83.4 12.7 %collective-permute-start.6 = (f32[256,512]{1,0:T(8,128)S(1)}, f32[256,512]{1,0:T(8,128)S(1)}, u32[]{:S(2)}, u32[]{:S(2)}) collective-permute-start(f32[256,512]{1,0:T(8,128)S(1)} %collective-permute-done.4.refs_5_), channel_id=1, source_target_pairs={{0,8},{8,16},{16,24},{24,32},{32,40},{40,48},{48,56},{56,0},{1,9},... | collective-permute-start | bytes 1572872 | tf_op jit(solution)/shard_map/ppermute | solution.py:42
  92.5 15.6 %collective-permute-start.7 = (f32[256,512]{1,0:T(8,128)}, f32[256,512]{1,0:T(8,128)S(1)}, u32[]{:S(2)}, u32[]{:S(2)}) collective-permute-start(f32[256,512]{1,0:T(8,128)} %collective-permute-done.5.refs_6_), channel_id=1, source_target_pairs={{0,56},{8,0},{16,8},{24,16},{32,24},{40,32},{48,40},{56,48},{1,57}... | collective-permute-start | bytes 1572872 | tf_op jit(solution)/shard_map/ppermute | solution.py:42
  96.1 0.8 copy-start.18
  108.2 0.8 copy-start.1
  112.5 62.3 %all-to-all-start.1 = ((f32[16,48,512]{2,1,0:T(8,128)}), f32[16,48,512]{2,1,0:T(8,128)S(1)}, u32[]{:S(2)}, u32[]{:S(2)}) async-start(f32[16,48,512]{2,1,0:T(8,128)} %bitcast.26), calls=%async_computation.1 | async-start | bytes 3145728 | tf_op jit(solution)/shard_map/all_to_all | solution.py:271
  120.4 37.3 %copy-start.3 = (f32[256,256]{1,0:T(8,128)}, f32[256,256]{1,0:T(8,128)S(1)}, u32[]{:S(2)}) copy-start(f32[256,256]{1,0:T(8,128)S(1)} %get-tuple-element.11.refs_7_) | copy-start | bytes 786436
  120.4 37.3 %copy-start.4 = (f32[256,256]{1,0:T(8,128)}, f32[256,256]{1,0:T(8,128)S(1)}, u32[]{:S(2)}) copy-start(f32[256,256]{1,0:T(8,128)S(1)} %get-tuple-element.12.refs_2_) | copy-start | bytes 786436
  120.4 9.1 %collective-permute-start.9 = (f32[256,256]{1,0:T(8,128)S(1)}, f32[256,256]{1,0:T(8,128)S(1)}, u32[]{:S(2)}, u32[]{:S(2)}) collective-permute-start(f32[256,256]{1,0:T(8,128)S(1)} %get-tuple-element.12.refs_2_), channel_id=1, source_target_pairs={{0,8},{8,16},{16,24},{24,32},{32,40},{40,48},{48,56},{56,0},{1,9},... | collective-permute-start | bytes 786440 | tf_op jit(solution)/shard_map/ppermute | solution.py:42
  120.7 14.5 %collective-permute-start.13 = (f32[256,256]{1,0:T(8,128)S(1)}, f32[256,256]{1,0:T(8,128)S(1)}, u32[]{:S(2)}, u32[]{:S(2)}) collective-permute-start(f32[256,256]{1,0:T(8,128)S(1)} %get-tuple-element.11.refs_7_), channel_id=1, source_target_pairs={{0,8},{8,16},{16,24},{24,32},{32,40},{40,48},{48,56},{56,0},{1,9},... | collective-permute-start | bytes 786440 | tf_op jit(solution)/shard_map/ppermute | solution.py:42
  120.8 14.4 %collective-permute-start.8 = (f32[256,256]{1,0:T(8,128)S(1)}, f32[256,256]{1,0:T(8,128)S(1)}, u32[]{:S(2)}, u32[]{:S(2)}) collective-permute-start(f32[256,256]{1,0:T(8,128)S(1)} %get-tuple-element.12.refs_2_), channel_id=1, source_target_pairs={{0,56},{8,0},{16,8},{24,16},{32,24},{40,32},{48,40},{56,48},{1,57}... | collective-permute-start | bytes 786440 | tf_op jit(solution)/shard_map/ppermute | solution.py:42
  123.5 14.4 %collective-permute-start.12 = (f32[256,256]{1,0:T(8,128)S(1)}, f32[256,256]{1,0:T(8,128)S(1)}, u32[]{:S(2)}, u32[]{:S(2)}) collective-permute-start(f32[256,256]{1,0:T(8,128)S(1)} %get-tuple-element.11.refs_7_), channel_id=1, source_target_pairs={{0,56},{8,0},{16,8},{24,16},{32,24},{40,32},{48,40},{56,48},{1,57}... | collective-permute-start | bytes 786440 | tf_op jit(solution)/shard_map/ppermute | solution.py:42
  129.6 28.1 %copy-start.19 = (f32[256,256]{1,0:T(8,128)}, f32[256,256]{1,0:T(8,128)S(1)}, u32[]{:S(2)}) copy-start(f32[256,256]{1,0:T(8,128)S(1)} %collective-permute-done.9.refs_4_) | copy-start | bytes 786436
  129.6 11.2 %collective-permute-start.11 = (f32[256,256]{1,0:T(8,128)S(1)}, f32[256,256]{1,0:T(8,128)S(1)}, u32[]{:S(2)}, u32[]{:S(2)}) collective-permute-start(f32[256,256]{1,0:T(8,128)S(1)} %collective-permute-done.9.refs_4_), channel_id=1, source_target_pairs={{0,8},{8,16},{16,24},{24,32},{32,40},{40,48},{48,56},{56,0},{1,9},... | collective-permute-start | bytes 786440 | tf_op jit(solution)/shard_map/ppermute | solution.py:42
  135.2 5.6 %copy-start.20 = (f32[256,256]{1,0:T(8,128)}, f32[256,256]{1,0:T(8,128)S(1)}, u32[]{:S(2)}) copy-start(f32[256,256]{1,0:T(8,128)S(1)} %collective-permute-done.13.refs_9_) | copy-start | bytes 786436
  135.2 11.2 %collective-permute-start.15 = (f32[256,256]{1,0:T(8,128)S(1)}, f32[256,256]{1,0:T(8,128)S(1)}, u32[]{:S(2)}, u32[]{:S(2)}) collective-permute-start(f32[256,256]{1,0:T(8,128)S(1)} %collective-permute-done.13.refs_9_), channel_id=1, source_target_pairs={{0,8},{8,16},{16,24},{24,32},{32,40},{40,48},{48,56},{56,0},{1,9},... | collective-permute-start | bytes 786440 | tf_op jit(solution)/shard_map/ppermute | solution.py:42
  135.2 11.2 %copy-start.21 = (f32[256,256]{1,0:T(8,128)}, f32[256,256]{1,0:T(8,128)S(1)}, u32[]{:S(2)}) copy-start(f32[256,256]{1,0:T(8,128)S(1)} %collective-permute-done.8.refs_3_) | copy-start | bytes 786436
  135.2 11.2 %collective-permute-start.10 = (f32[256,256]{1,0:T(8,128)S(1)}, f32[256,256]{1,0:T(8,128)}, u32[]{:S(2)}, u32[]{:S(2)}) collective-permute-start(f32[256,256]{1,0:T(8,128)S(1)} %collective-permute-done.8.refs_3_), channel_id=1, source_target_pairs={{0,56},{8,0},{16,8},{24,16},{32,24},{40,32},{48,40},{56,48},{1,57}... | collective-permute-start | bytes 786440 | tf_op jit(solution)/shard_map/ppermute | solution.py:42
  137.9 11.2 %copy-start.22 = (f32[256,256]{1,0:T(8,128)}, f32[256,256]{1,0:T(8,128)S(1)}, u32[]{:S(2)}) copy-start(f32[256,256]{1,0:T(8,128)S(1)} %collective-permute-done.12.refs_8_) | copy-start | bytes 786436
  137.9 11.2 %collective-permute-start.14 = (f32[256,256]{1,0:T(8,128)S(1)}, f32[256,256]{1,0:T(8,128)}, u32[]{:S(2)}, u32[]{:S(2)}) collective-permute-start(f32[256,256]{1,0:T(8,128)S(1)} %collective-permute-done.12.refs_8_), channel_id=1, source_target_pairs={{0,56},{8,0},{16,8},{24,16},{32,24},{40,32},{48,40},{56,48},{1,57}... | collective-permute-start | bytes 786440 | tf_op jit(solution)/shard_map/ppermute | solution.py:42
  140.8 9.9 %copy-start.23 = (f32[256,256]{1,0:T(8,128)}, f32[256,256]{1,0:T(8,128)S(1)}, u32[]{:S(2)}) copy-start(f32[256,256]{1,0:T(8,128)S(1)} %collective-permute-done.11.refs_6_) | copy-start | bytes 786436
  140.8 11.2 %collective-permute-start.17 = (f32[256,256]{1,0:T(8,128)S(1)}, f32[256,256]{1,0:T(8,128)S(1)}, u32[]{:S(2)}, u32[]{:S(2)}) collective-permute-start(f32[256,256]{1,0:T(8,128)S(1)} %collective-permute-done.11.refs_6_), channel_id=1, source_target_pairs={{0,8},{8,16},{16,24},{24,32},{32,40},{40,48},{48,56},{56,0},{1,9},... | collective-permute-start | bytes 786440 | tf_op jit(solution)/shard_map/ppermute | solution.py:42
  146.4 5.6 %copy-start.24 = (f32[256,256]{1,0:T(8,128)}, f32[256,256]{1,0:T(8,128)S(1)}, u32[]{:S(2)}) copy-start(f32[256,256]{1,0:T(8,128)S(1)} %collective-permute-done.15.refs_11_) | copy-start | bytes 786436
  146.4 11.2 %collective-permute-start.20 = (f32[256,256]{1,0:T(8,128)S(1)}, f32[256,256]{1,0:T(8,128)S(1)}, u32[]{:S(2)}, u32[]{:S(2)}) collective-permute-start(f32[256,256]{1,0:T(8,128)S(1)} %collective-permute-done.15.refs_11_), channel_id=1, source_target_pairs={{0,8},{8,16},{16,24},{24,32},{32,40},{40,48},{48,56},{56,0},{1,9},... | collective-permute-start | bytes 786440 | tf_op jit(solution)/shard_map/ppermute | solution.py:42
  146.5 17.8 %collective-permute-start.16 = (f32[256,256]{1,0:T(8,128)}, f32[256,256]{1,0:T(8,128)S(1)}, u32[]{:S(2)}, u32[]{:S(2)}) collective-permute-start(f32[256,256]{1,0:T(8,128)} %collective-permute-done.10.refs_5_), channel_id=1, source_target_pairs={{0,56},{8,0},{16,8},{24,16},{32,24},{40,32},{48,40},{56,48},{1,57}... | collective-permute-start | bytes 786440 | tf_op jit(solution)/shard_map/ppermute | solution.py:42
  149.1 15.2 %collective-permute-start.19 = (f32[256,256]{1,0:T(8,128)}, f32[256,256]{1,0:T(8,128)S(1)}, u32[]{:S(2)}, u32[]{:S(2)}) collective-permute-start(f32[256,256]{1,0:T(8,128)} %collective-permute-done.14.refs_10_), channel_id=1, source_target_pairs={{0,56},{8,0},{16,8},{24,16},{32,24},{40,32},{48,40},{56,48},{1,57}... | collective-permute-start | bytes 786440 | tf_op jit(solution)/shard_map/ppermute | solution.py:42
  152.1 12.2 %copy-start.5 = (f32[256,256]{1,0:T(8,128)}, f32[256,256]{1,0:T(8,128)S(1)}, u32[]{:S(2)}) copy-start(f32[256,256]{1,0:T(8,128)S(1)} %collective-permute-done.17.refs_5_) | copy-start | bytes 786436
  152.1 12.3 %collective-permute-start.18 = (f32[256,256]{1,0:T(8,128)S(1)}, f32[256,256]{1,0:T(8,128)S(1)}, u32[]{:S(2)}, u32[]{:S(2)}) collective-permute-start(f32[256,256]{1,0:T(8,128)S(1)} %collective-permute-done.17.refs_5_), channel_id=1, source_target_pairs={{0,8},{8,16},{16,24},{24,32},{32,40},{40,48},{48,56},{56,0},{1,9},... | collective-permute-start | bytes 786440 | tf_op jit(solution)/shard_map/ppermute | solution.py:42
  157.7 6.6 %copy-start.6 = (f32[256,256]{1,0:T(8,128)}, f32[256,256]{1,0:T(8,128)S(1)}, u32[]{:S(2)}) copy-start(f32[256,256]{1,0:T(8,128)S(1)} %collective-permute-done.20.refs_8_) | copy-start | bytes 786436
  157.7 11.2 %collective-permute-start.21 = (f32[256,256]{1,0:T(8,128)S(1)}, f32[256,256]{1,0:T(8,128)S(1)}, u32[]{:S(2)}, u32[]{:S(2)}) collective-permute-start(f32[256,256]{1,0:T(8,128)S(1)} %collective-permute-done.20.refs_8_), channel_id=1, source_target_pairs={{0,8},{8,16},{16,24},{24,32},{32,40},{40,48},{48,56},{56,0},{1,9},... | collective-permute-start | bytes 786440 | tf_op jit(solution)/shard_map/ppermute | solution.py:42
  164.3 4.6 %copy-start.7 = (f32[256,256]{1,0:T(8,128)}, f32[256,256]{1,0:T(8,128)S(1)}, u32[]{:S(2)}) copy-start(f32[256,256]{1,0:T(8,128)S(1)} %collective-permute-done.16.refs_4_) | copy-start | bytes 786436
  164.3 4.6 %copy-start.8 = (f32[256,256]{1,0:T(8,128)}, f32[256,256]{1,0:T(8,128)S(1)}, u32[]{:S(2)}) copy-start(f32[256,256]{1,0:T(8,128)S(1)} %collective-permute-done.19.refs_7_) | copy-start | bytes 786436
  164.3 4.6 %copy-start.9 = (f32[256,256]{1,0:T(8,128)}, f32[256,256]{1,0:T(8,128)S(1)}, u32[]{:S(2)}) copy-start(f32[256,256]{1,0:T(8,128)S(1)} %collective-permute-done.18.refs_6_) | copy-start | bytes 786436
  168.9 0.7 copy-start.10
  174.8 6.4 %copy-start.13 = (s32[48,2]{0,1:T(2,128)S(1)}, s32[48,2]{0,1:T(2,128)}, u32[]{:S(2)}) copy-start(s32[48,2]{0,1:T(2,128)} %param.7) | copy-start | bytes 1156
  174.8 6.4 %copy-start.12 = (f32[200]{0:T(256)S(1)}, f32[200]{0:T(256)}, u32[]{:S(2)}) copy-start(f32[200]{0:T(256)} %param.8) | copy-start | bytes 2404
  174.8 28.2 %all-to-all-start.2 = ((f32[16,48,512]{2,1,0:T(8,128)}), f32[16,48,512]{2,1,0:T(8,128)S(1)}, u32[]{:S(2)}, u32[]{:S(2)}) async-start(f32[16,48,512]{2,1,0:T(8,128)} %bitcast.27), calls=%async_computation.2 | async-start | bytes 3145728 | tf_op jit(solution)/shard_map/all_to_all | solution.py:271
  181.4 21.9 %copy-start.11 = (f32[2048]{0:T(1024)S(1)}, f32[2048]{0:T(1024)}, u32[]{:S(2)}) copy-start(f32[2048]{0:T(1024)} %param.9) | copy-start | bytes 24580
